TPU v7x, 128 devices: a whole 4x4x4 slice. The times are simulated.
128 devices in a mesh: pool: 4 (over x_hi, core), dp: 32 (over z, x_lo, y).
Axes of the slice: x: 4 (x_hi: 2, x_lo: 2; x = x_hi * 2 + x_lo), y: 4, z: 4, core: 2. Of those that a mesh axis runs over, the one named last changes fastest.
Arguments:
- queries: bfloat16 [4, 32, 256, 2048], P('pool', 'dp'), may hold values from -48 to 48
- cotangent: bfloat16 [4, 32, 256, 2048], P('pool', 'dp'), may hold values from -6 to 6
- cond: bfloat16 [4, 32, 4, 512], P('pool', 'dp'), may hold values from -6 to 6
- nbr_owner: int32 [4, 32, 4, 2], P('pool', 'dp'), may hold values from 0 to 31, as said below
- nbr_block: int32 [4, 32, 4, 2], P('pool', 'dp'), may hold values from 0 to 15
- database: bfloat16 [4, 32, 16, 128, 512], P('pool', 'dp'), may hold values from -6 to 6
- lengths: int32 [4, 32, 16], P('pool', 'dp'), may hold values from 1 to 128, as said below
- gain: float32 [512], replicated, may hold values from 0.25 to 1.75
- w_down: bfloat16 [512, 256], replicated, may hold values from -0.25 to 0.25
- w_up: bfloat16 [256, 512], replicated, may hold values from -0.375 to 0.375
- w_kv: bfloat16 [512, 4096], replicated, may hold values from -0.25 to 0.25
Outputs:
- attn_out: bfloat16 [4, 32, 256, 2048], P('pool', 'dp')
- q_grad: bfloat16 [4, 32, 256, 2048], P('pool', 'dp')
- cond_grad: float32 [4, 32, 4, 512], P('pool', 'dp')
- adapter_grad: float32 [512, 512], P(('pool', 'dp'))
Inputs may be any that keep to these rules, and one draw needn't show every extreme that they name: `nbr_owner`: among the 8 neighbours of each of the decoder devices (pool index below 4-1) that share one index of dp, no encoder device is named more than 2 times, and one encoder device, the same for every index of dp, is named exactly 2 times. Entries at pool index 4-1 are not read. `lengths`: every encoder device holds a block of length 128.
All inputs are finite; a program needn't handle non-finite values.
Results may differ from a plain program's by a relative error of at most 0.013.
The roundings to bfloat16 on the way count: a program that leaves them out, or rounds other values in their place, can miss the bound.
Values may be sent and summed in bfloat16 or wider, within the bound.
A program may use at most 192 MiB of HBM per device.

v0:
```python
import jax
import jax.numpy as jnp
from jax import lax
from jax.sharding import PartitionSpec as P

HEADS = 16
HEAD = 128
SPAN = 64


EPSILON = 1e-06
FLOOR = -1e30


def spread(block, axis, owner):
    block = jnp.where(lax.axis_index(axis) == owner, block, jnp.zeros_like(block))
    return lax.psum(block, axis)


def encode_rows(block_rows, cond_rows, gain, w_down, w_up):
    x_full = block_rows.astype(jnp.float32) + cond_rows.astype(jnp.float32)[..., None, :]
    inv_rms = lax.rsqrt(jnp.mean(x_full * x_full, axis=-1, keepdims=True) + EPSILON)
    hidden = (x_full * inv_rms * gain).astype(jnp.bfloat16)
    flat_hidden = hidden.reshape(-1, hidden.shape[-1])
    latent = jnp.dot(flat_hidden, w_down, preferred_element_type=jnp.float32).astype(jnp.bfloat16)
    branch = jnp.dot(latent, w_up, preferred_element_type=jnp.float32).reshape(x_full.shape)
    encoded = (x_full + branch).astype(jnp.bfloat16)
    return (
        encoded,
        x_full,
        inv_rms,
        hidden,
        latent.reshape(x_full.shape[:-1] + (latent.shape[-1],)),
    )


def encode_back(enc_grad, x_full, inv_rms, gain, w_down, w_up):
    flat_grad = enc_grad.reshape(-1, enc_grad.shape[-1])
    lat_grad = jnp.dot(flat_grad, w_up.T, preferred_element_type=jnp.float32).astype(jnp.bfloat16)
    hid_grad = jnp.dot(lat_grad, w_down.T, preferred_element_type=jnp.float32).reshape(x_full.shape)
    scaled = hid_grad * gain
    normed = x_full * inv_rms
    x_grad = enc_grad.astype(jnp.float32) + inv_rms * (
        scaled - normed * jnp.mean(scaled * normed, axis=-1, keepdims=True)
    )
    return (jnp.sum(x_grad, axis=-2), lat_grad.reshape(x_full.shape[:-1] + (lat_grad.shape[-1],)))


def attend(query_rows, cot_rows, encoded, block_len, w_kv):
    token_count, head_cols = query_rows.shape
    block_count, slot_len, enc_width = encoded.shape
    span_count = token_count // SPAN
    key_count = block_count * slot_len // span_count
    scaling = HEAD ** (-0.5)
    key_value = jnp.dot(
        encoded.reshape(block_count * slot_len, enc_width), w_kv, preferred_element_type=jnp.float32
    ).astype(jnp.bfloat16)
    key_rows = key_value[:, :head_cols].reshape(span_count, key_count, HEADS, HEAD)
    value_rows = key_value[:, head_cols:].reshape(span_count, key_count, HEADS, HEAD)
    q_heads = query_rows.reshape(span_count, SPAN, HEADS, HEAD)
    out_grad = cot_rows.reshape(span_count, SPAN, HEADS, HEAD)
    usable = (jnp.arange(slot_len, dtype=jnp.int32)[None, :] < block_len[:, None]).reshape(
        span_count, 1, 1, key_count
    )
    scores = (
        jnp.einsum("cqhd,ckhd->chqk", q_heads, key_rows, preferred_element_type=jnp.float32)
        * scaling
    )
    scores = jnp.where(usable, scores, FLOOR)
    row_max = jnp.max(scores, axis=-1, keepdims=True)
    raised = jnp.exp(scores - row_max)
    probs = raised / jnp.sum(raised, axis=-1, keepdims=True)
    probs_b = probs.astype(jnp.bfloat16)
    attn_out = (
        jnp.einsum("chqk,ckhd->cqhd", probs_b, value_rows, preferred_element_type=jnp.float32)
        .astype(jnp.bfloat16)
        .reshape(token_count, head_cols)
    )
    d_probs = jnp.einsum(
        "cqhd,ckhd->chqk", out_grad, value_rows, preferred_element_type=jnp.float32
    )
    delta = jnp.sum(probs * d_probs, axis=-1, keepdims=True)
    d_scores = (probs * (d_probs - delta)).astype(jnp.bfloat16)
    q_grad = (
        (
            jnp.einsum("chqk,ckhd->cqhd", d_scores, key_rows, preferred_element_type=jnp.float32)
            * scaling
        )
        .astype(jnp.bfloat16)
        .reshape(token_count, head_cols)
    )
    key_grad = (
        jnp.einsum("chqk,cqhd->ckhd", d_scores, q_heads, preferred_element_type=jnp.float32)
        * scaling
    ).astype(jnp.bfloat16)
    value_grad = jnp.einsum(
        "chqk,cqhd->ckhd", probs_b, out_grad, preferred_element_type=jnp.float32
    ).astype(jnp.bfloat16)
    kv_grad = jnp.concatenate(
        [
            key_grad.reshape(block_count * slot_len, head_cols),
            value_grad.reshape(block_count * slot_len, head_cols),
        ],
        axis=1,
    )
    enc_grad = lax.dot_general(
        kv_grad, w_kv, (((1,), (1,)), ((), ())), preferred_element_type=jnp.float32
    ).astype(jnp.bfloat16)
    return (attn_out, q_grad, enc_grad.reshape(block_count, slot_len, enc_width))


def body(
    queries, cotangent, cond, nbr_owner, nbr_block, database, lengths, gain, w_down, w_up, w_kv
):
    pool_count = lax.axis_size("pool")
    columns = lax.axis_size("dp")
    relay_row = pool_count - 1
    pool_index = lax.axis_index("pool")
    on_encoder = pool_index == relay_row
    span_count = cond.shape[2]
    enc_width = cond.shape[3]
    nbr_count = nbr_owner.shape[3]
    per_device = span_count * nbr_count
    slot_len = database.shape[3]
    live_count = relay_row * per_device
    capacity = max(2, live_count // columns + 1)
    slot_count = columns * capacity
    token_count = queries.shape[2]
    head_cols = queries.shape[3]
    rank_width = w_down.shape[1]
    lead_shape = (columns, capacity, slot_len)
    owners_all, blocks_all, conds_all = (
        lax.all_gather(nbr_owner.reshape(1, per_device), "pool", axis=0, tiled=True),
        lax.all_gather(nbr_block.reshape(1, per_device), "pool", axis=0, tiled=True),
        lax.all_gather(cond.reshape(1, span_count, enc_width), "pool", axis=0, tiled=True),
    )
    req_owner = owners_all[:relay_row].reshape(live_count)
    req_block = blocks_all[:relay_row].reshape(live_count)
    owner_hot = (req_owner[:, None] == jnp.arange(columns, dtype=jnp.int32)[None, :]).astype(
        jnp.int32
    )
    slot_rank = jnp.sum(jnp.cumsum(owner_hot, axis=0) * owner_hot, axis=1) - 1
    position = (req_owner * capacity + slot_rank).astype(jnp.int32)
    placing = jnp.arange(slot_count, dtype=jnp.int32)[:, None] == position[None, :]
    placing_b = placing.astype(jnp.bfloat16)
    slot_block = (
        jnp.sum(jnp.where(placing, req_block[None, :], 0), axis=1)
        .astype(jnp.int32)
        .reshape(columns, capacity)
    )
    req_cond = jnp.repeat(conds_all[:relay_row], nbr_count, axis=1).reshape(live_count, enc_width)
    slot_cond = (
        jnp.dot(placing_b, req_cond, preferred_element_type=jnp.float32)
        .astype(jnp.bfloat16)
        .reshape(columns, capacity, enc_width)
    )
    got_block, got_cond = (
        lax.all_to_all(slot_block, "dp", split_axis=0, concat_axis=0, tiled=True),
        lax.all_to_all(slot_cond, "dp", split_axis=0, concat_axis=0, tiled=True),
    )
    store_rows = database.reshape(database.shape[2], slot_len, enc_width)
    store_len = lengths.reshape(lengths.shape[2])
    flat_block = got_block.reshape(slot_count)
    block_rows = jnp.take(store_rows, flat_block, axis=0).reshape(lead_shape + (enc_width,))
    block_hot = flat_block[:, None] == jnp.arange(store_len.shape[0], dtype=jnp.int32)[None, :]
    row_len = jnp.sum(jnp.where(block_hot, store_len[None, :], 0), axis=1).reshape(
        columns, capacity
    )

    def encode_all(rows_in, cond_in):
        return encode_rows(rows_in, cond_in, gain, w_down, w_up)

    def encode_none(rows_in, cond_in):
        return (
            jnp.zeros(lead_shape + (enc_width,), jnp.bfloat16),
            jnp.zeros(lead_shape + (enc_width,), jnp.float32),
            jnp.zeros(lead_shape + (1,), jnp.float32),
            jnp.zeros(lead_shape + (enc_width,), jnp.bfloat16),
            jnp.zeros(lead_shape + (rank_width,), jnp.bfloat16),
        )

    encoded, x_full, inv_rms, hidden, latent = lax.cond(
        on_encoder, encode_all, encode_none, block_rows, got_cond
    )
    back_enc, back_len = (
        lax.all_to_all(encoded, "dp", split_axis=0, concat_axis=0, tiled=True),
        lax.all_to_all(row_len, "dp", split_axis=0, concat_axis=0, tiled=True),
    )
    mine_enc = jnp.take(
        back_enc.reshape(slot_count, slot_len, enc_width), position, axis=0
    ).reshape(relay_row, per_device, slot_len, enc_width)
    mine_len = jnp.take(back_len.reshape(slot_count), position, axis=0).reshape(
        relay_row, per_device
    )
    down_enc, down_len = (spread(mine_enc, "pool", relay_row), spread(mine_len, "pool", relay_row))
    own_row = jnp.minimum(pool_index, relay_row - 1)
    my_enc = lax.dynamic_index_in_dim(down_enc, own_row, 0, keepdims=False)
    my_len = lax.dynamic_index_in_dim(down_len, own_row, 0, keepdims=False)
    query_flat = queries.reshape(token_count, head_cols)
    cot_flat = cotangent.reshape(token_count, head_cols)

    def decode_run(query_rows, cot_rows, enc_rows, len_rows):
        return attend(query_rows, cot_rows, enc_rows, len_rows, w_kv)

    def decode_skip(query_rows, cot_rows, enc_rows, len_rows):
        return (
            jnp.zeros((token_count, head_cols), jnp.bfloat16),
            jnp.zeros((token_count, head_cols), jnp.bfloat16),
            jnp.zeros((per_device, slot_len, enc_width), jnp.bfloat16),
        )

    attn_out, q_grad, enc_grad = lax.cond(
        on_encoder, decode_skip, decode_run, query_flat, cot_flat, my_enc, my_len
    )
    up_grads = lax.all_gather(enc_grad[None], "pool", axis=0, tiled=True)
    flat_up = up_grads[:relay_row].reshape(live_count, slot_len * enc_width)
    slot_grads = (
        jnp.dot(placing_b, flat_up, preferred_element_type=jnp.float32)
        .astype(jnp.bfloat16)
        .reshape(lead_shape + (enc_width,))
    )
    got_grads = lax.all_to_all(slot_grads, "dp", split_axis=0, concat_axis=0, tiled=True)

    def owner_back(grad_in, x_in, rms_in, hid_in, lat_in):
        cond_rows_grad, lat_grad = encode_back(grad_in, x_in, rms_in, gain, w_down, w_up)
        return (cond_rows_grad, lat_grad, hid_in, lat_in)

    back_args = (got_grads, x_full, inv_rms, hidden, latent)

    def owner_skip(*unused):
        return (
            jnp.zeros((columns, capacity, enc_width), jnp.float32),
            jnp.zeros(lead_shape + (rank_width,), jnp.bfloat16),
            jnp.zeros(lead_shape + (enc_width,), jnp.bfloat16),
            jnp.zeros(lead_shape + (rank_width,), jnp.bfloat16),
        )

    cond_rows_grad, lat_grad, hid_used, lat_used = lax.cond(
        on_encoder, owner_back, owner_skip, *back_args
    )
    term_rows = slot_count * slot_len
    flat_hidden = hid_used.reshape(term_rows, enc_width)
    flat_latgrad = lat_grad.reshape(term_rows, rank_width)
    flat_grads = got_grads.reshape(term_rows, enc_width)
    flat_latent = lat_used.reshape(term_rows, rank_width)
    cond_back = lax.all_to_all(
        cond_rows_grad.astype(jnp.bfloat16), "dp", split_axis=0, concat_axis=0, tiled=True
    ).astype(cond_rows_grad.dtype)
    mine_cond = jnp.take(cond_back.reshape(slot_count, enc_width), position, axis=0).reshape(
        relay_row, span_count, nbr_count, enc_width
    )
    mine_cond = jnp.sum(mine_cond, axis=2)
    down_cond = spread(mine_cond, "pool", relay_row)
    my_cond = lax.dynamic_index_in_dim(
        down_cond, jnp.minimum(pool_index, relay_row - 1), 0, keepdims=False
    )
    my_cond = jnp.where(on_encoder, jnp.zeros_like(my_cond), my_cond)

    def compute(unused):
        down_part = lax.dot_general(
            flat_hidden, flat_latgrad, (((0,), (0,)), ((), ())), preferred_element_type=jnp.float32
        )
        up_part = lax.dot_general(
            flat_grads, flat_latent, (((0,), (0,)), ((), ())), preferred_element_type=jnp.float32
        )
        return jnp.concatenate([down_part, up_part], axis=1)

    def nothing(unused):
        return jnp.zeros(
            (enc_width // (pool_count * columns) * lax.axis_size(("pool", "dp")), 2 * rank_width),
            jnp.float32,
        )

    adapter_grad = lax.psum_scatter(
        lax.cond(on_encoder, compute, nothing, 0), ("pool", "dp"), scatter_dimension=0, tiled=True
    )
    return (
        attn_out.reshape(1, 1, token_count, head_cols),
        q_grad.reshape(1, 1, token_count, head_cols),
        my_cond.reshape(1, 1, span_count, enc_width),
        adapter_grad,
    )


def solution(mesh):
    return jax.shard_map(
        body,
        mesh=mesh,
        in_specs=(
            P("pool", "dp", None, None),
            P("pool", "dp", None, None),
            P("pool", "dp", None, None),
            P("pool", "dp", None, None),
            P("pool", "dp", None, None),
            P("pool", "dp", None, None, None),
            P("pool", "dp", None),
            P(),
            P(),
            P(),
            P(),
        ),
        out_specs=(
            P("pool", "dp", None, None),
            P("pool", "dp", None, None),
            P("pool", "dp", None, None),
            P(("pool", "dp"), None),
        ),
        check_vma=False,
    )
```

profile of v0, /device:TPU:1, one launch (start us, length us, event | category | flops | bytes accessed | tf_op | source)
XLA Modules:
  0.0 751.4 jit_solution(18239631943849890911)
XLA Ops:
  8.0 7.8 %all-gather.2 = s32[4,1,8]{2,1,0:T(1,128)S(1)} all-gather(s32[1,1,8]{2,1,0:T(1,128)S(1)} %reshape.437), channel_id=1, replica_groups=mesh['pool'=4,'dp'=32] {'pool'}, dimensions={0}, use_global_device_ids=true | all-gather | bytes 160 | tf_op jit(solution)/shard_map/all_gather | solution.py:133
  17.1 6.6 all-gather.3
  24.5 9.1 %all-to-all-start = ((s32[32,1,2]{2,1,0:T(1,128)}), s32[32,1,2]{2,1,0:T(1,128)S(1)}, u32[]{:S(2)}, u32[]{:S(2)}) async-start(s32[32,1,2]{2,1,0:T(1,128)} %bitcast.27), calls=%async_computation | async-start | bytes 32768 | tf_op jit(solution)/shard_map/all_to_all | solution.py:158
  33.6 7.1 all-gather
  41.8 8.0 %all-to-all-start.2 = ((bf16[32,2,512]{2,1,0:T(2,128)(2,1)}), bf16[32,2,512]{2,1,0:T(2,128)(2,1)S(1)}, u32[]{:S(2)}, u32[]{:S(2)}) async-start(bf16[32,2,512]{2,1,0:T(2,128)(2,1)} %reshape.392), calls=%async_computation.2 | async-start | bytes 131072 | tf_op jit(solution)/shard_map/all_to_all | solution.py:159
  61.0 19.3 %conditional.4 = (bf16[32,2,128,512]{3,2,1,0:T(8,128)(2,1)}, f32[32,2,128,512]{3,2,1,0:T(8,128)}, f32[32,2,128,1]{2,1,0,3:T(2,128)S(1)}, bf16[32,2,128,512]{3,2,1,0:T(8,128)(2,1)}, bf16[32,2,128,256]{3,2,1,0:T(8,128)(2,1)}) conditional(s32[]{:T(128)} %convert_element_type.123, () %tuple.63, (s32[64]{0:T(128)S(1)}, ...), branch_computations={%region_3.4_spmd, %region_4.6_spmd} | conditional | flops 4376798720 | bytes 154913088 | solution.py:182
  61.0 7.9 %broadcast.330 = f32[32,2,128,512]{3,2,1,0:T(8,128)} broadcast(f32[]{:T(128)} %constant.132.clone), dimensions={} | broadcast | bytes 16777220 | tf_op jit(solution)/shard_map/broadcast.9
  80.2 7.9 %all-to-all-start.3 = ((bf16[32,2,128,512]{3,2,1,0:T(8,128)(2,1)}), bf16[32,2,128,512]{3,2,1,0:T(8,128)(2,1)}, u32[]{:S(2)}, u32[]{:S(2)}) async-start(bf16[32,2,128,512]{3,2,1,0:T(8,128)(2,1)} %get-tuple-element.250), calls=%async_computation.3 | async-start | bytes 16777216 | tf_op jit(solution)/shard_map/all_to_all | solution.py:186
  90.5 104.1 %all-to-all-done.3 = bf16[32,2,128,512]{3,2,1,0:T(8,128)(2,1)} async-done(((bf16[32,2,128,512]{3,2,1,0:T(8,128)(2,1)}), bf16[32,2,128,512]{3,2,1,0:T(8,128)(2,1)}, u32[]{:S(2)}, u32[]{:S(2)}) %all-to-all-start.3) | async-done | bytes 8388640 | tf_op jit(solution)/shard_map/all_to_all | solution.py:186
  200.9 10.0 %psum.21 = s32[3,8]{1,0:T(4,128)S(1)} all-reduce(s32[3,8]{1,0:T(4,128)S(1)} %get-tuple-element.293), channel_id=1, replica_groups=mesh['pool'=4,'dp'=32] {'pool'}, use_global_device_ids=true, to_apply=%region_8.9 | all-reduce | flops 24 | bytes 192 | tf_op jit(solution)/shard_map/psum | solution.py:17
  211.0 83.4 %all-reduce.4.cloned.1.call-done = bf16[3,8,128,512]{3,2,1,0:T(8,128)(2,1)} async-done(((bf16[3,8,128,512]{3,2,1,0:T(8,128)(2,1)}), bf16[3,8,128,512]{3,2,1,0:T(8,128)(2,1)}) %all-reduce.4.cloned.1.call-update) | async-done | bytes 3145744 | tf_op jit(solution)/shard_map/psum | solution.py:17
  294.3 58.2 %conditional.5 = (bf16[8,128,512]{2,1,0:T(8,128)(2,1)S(1)}, bf16[1,1,256,2048]{3,2,1,0:T(8,128)(2,1)S(1)}, bf16[1,1,256,2048]{3,2,1,0:T(8,128)(2,1)}) conditional(s32[]{:T(128)} %convert_element_type.123, (s32[3,8]{1,0:T(4,128)S(1)}, s32[]{:T(128)}, bf16[3,8,128,512]{3,2,1,0:T(8,128)(2,1)}, bf16[512,4096]{1,0:T(8,128)(2,1)}, ...), branch_computations={%region_9.13_spmd, %region_13.14_spmd} | conditional | flops 10247730176 | bytes 318894592 | solution.py:212
  295.7 6.9 convolution_convert_fusion.2
  342.7 6.9 fusion.31
  353.6 37.9 %all-gather.6.cloned.1.call-done = bf16[32,128,512]{2,1,0:T(8,128)(2,1)} async-done(((bf16[8,128,512]{2,1,0:T(8,128)(2,1)}), bf16[32,128,512]{2,1,0:T(8,128)(2,1)}) %all-gather.6.cloned.1.call-update) | async-done | bytes 4194320 | tf_op jit(solution)/shard_map/all_gather | solution.py:215
  395.2 5.7 convolution_convert_fusion.3
  400.8 9.9 %copy.133 = bf16[8,8,128,512]{3,2,1,0:T(8,128)(2,1)} copy(bf16[8,8,128,512]{3,1,2,0:T(8,128)(2,1)} %bitcast.152) | data formatting | bytes 16777216
  410.7 7.3 all-to-all-start.4
  418.2 117.5 %all-to-all-done.4 = bf16[32,2,128,512]{3,2,1,0:T(8,128)(2,1)} async-done(((bf16[32,2,128,512]{3,2,1,0:T(8,128)(2,1)}), bf16[32,2,128,512]{3,2,1,0:T(8,128)(2,1)}, u32[]{:S(2)}, u32[]{:S(2)}) %all-to-all-start.4) | async-done | bytes 8388640 | tf_op jit(solution)/shard_map/all_to_all | solution.py:222
  535.8 7.1 conditional.6
  544.4 23.7 %all-to-all-start.5 = ((bf16[32,2,512]{2,1,0:T(2,128)(2,1)}), bf16[32,2,512]{2,1,0:T(2,128)(2,1)S(1)}, u32[]{:S(2)}, u32[]{:S(2)}) async-start(bf16[32,2,512]{2,1,0:T(2,128)(2,1)} %get-tuple-element.258), calls=%async_computation.5 | async-start | bytes 131072 | tf_op jit(solution)/shard_map/all_to_all | solution.py:246
  568.2 7.1 all-to-all-done.5
  576.1 45.8 %psum.23 = f32[3,4,512]{2,1,0:T(4,128)S(1)} all-reduce(f32[3,4,512]{2,1,0:T(4,128)S(1)} %broadcast_select_fusion), channel_id=1, replica_groups=mesh['pool'=4,'dp'=32] {'pool'}, use_global_device_ids=true, to_apply=%region_19.20 | all-reduce | flops 6144 | bytes 49152 | tf_op jit(solution)/shard_map/psum | solution.py:17
  622.5 120.8 %all-reduce.6.cloned.1.call-done = f32[512,512]{1,0:T(8,128)} async-done(((f32[512,512]{1,0:T(8,128)}), f32[512,512]{1,0:T(8,128)}) %all-reduce.6.cloned.1.call-update) | async-done | bytes 1048592
  (131 shorter events, 94.9 us)
Async XLA Ops:
  24.5 17.2 %all-to-all-start = ((s32[32,1,2]{2,1,0:T(1,128)}), s32[32,1,2]{2,1,0:T(1,128)S(1)}, u32[]{:S(2)}, u32[]{:S(2)}) async-start(s32[32,1,2]{2,1,0:T(1,128)} %bitcast.27), calls=%async_computation | async-start | bytes 32768 | tf_op jit(solution)/shard_map/all_to_all | solution.py:158
  41.8 15.4 %all-to-all-start.2 = ((bf16[32,2,512]{2,1,0:T(2,128)(2,1)}), bf16[32,2,512]{2,1,0:T(2,128)(2,1)S(1)}, u32[]{:S(2)}, u32[]{:S(2)}) async-start(bf16[32,2,512]{2,1,0:T(2,128)(2,1)} %reshape.392), calls=%async_computation.2 | async-start | bytes 131072 | tf_op jit(solution)/shard_map/all_to_all | solution.py:159
  57.1 23.1 %all-to-all-start.1 = ((s32[32,1,2]{2,1,0:T(1,128)}), s32[32,1,2]{2,1,0:T(1,128)S(1)}, u32[]{:S(2)}, u32[]{:S(2)}) async-start(s32[32,1,2]{2,1,0:T(1,128)} %bitcast.29), calls=%async_computation.1 | async-start | bytes 32768 | tf_op jit(solution)/shard_map/all_to_all | solution.py:187
  80.2 114.4 %all-to-all-start.3 = ((bf16[32,2,128,512]{3,2,1,0:T(8,128)(2,1)}), bf16[32,2,128,512]{3,2,1,0:T(8,128)(2,1)}, u32[]{:S(2)}, u32[]{:S(2)}) async-start(bf16[32,2,128,512]{3,2,1,0:T(8,128)(2,1)} %get-tuple-element.250), calls=%async_computation.3 | async-start | bytes 16777216 | tf_op jit(solution)/shard_map/all_to_all | solution.py:186
  88.1 206.2 %all-reduce.4.cloned.1.call-start = ((), (), s32[]{:S(2)}) async-start(), calls=%async_computation.6 | async-start | bytes 6291456 | tf_op jit(solution)/shard_map/psum | solution.py:17
  200.8 190.7 %all-gather.6.cloned.1.call-start = ((), (), s32[]{:S(2)}) async-start(), calls=%async_computation.7 | async-start | bytes 5242880 | tf_op jit(solution)/shard_map/all_gather | solution.py:215
  306.5 3.8 copy-start
  310.5 5.4 copy-start.2
  315.9 4.8 copy-start.5
  315.9 2.0 copy-start.10
  317.3 3.4 copy-start.7
  318.1 2.5 copy-start.11
  320.7 2.2 copy-start.1
  330.2 2.7 copy-start.6
  330.2 2.7 copy-start.12
  342.7 6.9 copy-start.8
  352.6 42.6 %copy-start.14 = (bf16[1,1,256,2048]{3,2,1,0:T(8,128)(2,1)}, bf16[1,1,256,2048]{3,2,1,0:T(8,128)(2,1)S(1)}, u32[]{:S(2)}) copy-start(bf16[1,1,256,2048]{3,2,1,0:T(8,128)(2,1)S(1)} %get-tuple-element.246) | copy-start | bytes 3145732
  391.5 1.9 slice-start
  410.7 125.0 %copy-start.17 = (bf16[512,256]{1,0:T(8,128)(2,1)S(1)}, bf16[512,256]{1,0:T(8,128)(2,1)}, u32[]{:S(2)}) copy-start(bf16[512,256]{1,0:T(8,128)(2,1)} %param.27) | copy-start | bytes 786436
  410.7 125.0 %copy-start.19 = (bf16[256,512]{1,0:T(8,128)(2,1)S(1)}, bf16[256,512]{1,0:T(8,128)(2,1)}, u32[]{:S(2)}) copy-start(bf16[256,512]{1,0:T(8,128)(2,1)} %param.28) | copy-start | bytes 786436
  410.7 125.0 %copy-start.21 = (f32[512]{0:T(512)S(1)}, f32[512]{0:T(512)}, u32[]{:S(2)}) copy-start(f32[512]{0:T(512)} %param.26) | copy-start | bytes 6148
  410.7 125.0 %all-to-all-start.4 = ((bf16[32,2,128,512]{3,2,1,0:T(8,128)(2,1)}), bf16[32,2,128,512]{3,2,1,0:T(8,128)(2,1)}, u32[]{:S(2)}, u32[]{:S(2)}) async-start(bf16[32,2,128,512]{3,2,1,0:T(8,128)(2,1)} %bitcast.151), calls=%async_computation.4 | async-start | bytes 16777216 | tf_op jit(solution)/shard_map/all_to_all | solution.py:222
  418.0 325.3 %all-reduce.6.cloned.1.call-start = ((), (), s32[]{:S(2)}) async-start(), calls=%async_computation.8 | async-start | bytes 2097152
  544.4 30.9 %all-to-all-start.5 = ((bf16[32,2,512]{2,1,0:T(2,128)(2,1)}), bf16[32,2,512]{2,1,0:T(2,128)(2,1)S(1)}, u32[]{:S(2)}, u32[]{:S(2)}) async-start(bf16[32,2,512]{2,1,0:T(2,128)(2,1)} %get-tuple-element.258), calls=%async_computation.5 | async-start | bytes 131072 | tf_op jit(solution)/shard_map/all_to_all | solution.py:246
  (2 other events, 2.4 us)
Sparse Core Ops, SparseCore 0:
  201.0 93.3 all-reduce.3
  353.7 37.7 all-gather.5
  544.5 198.7 all-reduce.5
where the time goes:
time: 757 us; the launch traced here: 751 us
  waiting for transfers between devices  475 us (63%)
  local copies, waits for them, and re-layouts  78.1 us (10%)
  blocking collectives  77.3 us (10%)
  starting transfers between devices  60.3 us (8%)
  matrix products  32.9 us (4%)
  between operations  14.2 us (2%)
  other arithmetic  12 us (2%)
    unnamed x4, waiting for transfers between devices  121 us
    all_to_all x1, waiting for transfers between devices, body(): lax.all_to_all(slot_grads, 'dp', split_axis=0, concat_axis=0, tiled=True)  118 us
    all_to_all x1, waiting for transfers between devices, body(): lax.all_to_all(encoded, 'dp', split_axis=0, concat_axis=0, tiled=True)  104 us
    psum x1, waiting for transfers between devices, spread(): return lax.psum(block, axis)  83.4 us
    psum x2, blocking collectives, spread(): return lax.psum(block, axis)  55.8 us
    all_gather x1, waiting for transfers between devices, body(): up_grads = lax.all_gather(enc_grad[None], 'pool', axis=0, tiled=True)  37.9 us
    all_to_all x1, starting transfers between devices, body(): lax.all_to_all(cond_rows_grad.astype(jnp.bfloat16), 'dp', split_axis=0, c...  23.7 us
    another operation x7, local copies, waits for them, and re-layouts  19.5 us
  transfers between devices with their start and end apart: 9, of which 7 were waited for; matrix products, arithmetic and copies ran while one was open for 3% of the time, Pallas kernels for 0%

commit v1 on v0

v1 whole, which is shorter than its diff:
```python
import jax
import jax.numpy as jnp
from jax import lax
from jax.sharding import PartitionSpec as P

HEADS = 16
HEAD = 128
SPAN = 64
EPSILON = 1e-06
FLOOR = -1e30


def encode_rows(block_rows, cond_rows, gain, w_down, w_up):
    x_full = block_rows.astype(jnp.float32) + cond_rows.astype(jnp.float32)[..., None, :]
    inv_rms = lax.rsqrt(jnp.mean(x_full * x_full, axis=-1, keepdims=True) + EPSILON)
    hidden = (x_full * inv_rms * gain).astype(jnp.bfloat16)
    flat_hidden = hidden.reshape(-1, hidden.shape[-1])
    latent = jnp.dot(flat_hidden, w_down, preferred_element_type=jnp.float32).astype(jnp.bfloat16)
    branch = jnp.dot(latent, w_up, preferred_element_type=jnp.float32).reshape(x_full.shape)
    encoded = (x_full + branch).astype(jnp.bfloat16)
    return encoded, x_full, inv_rms, flat_hidden, latent


def encode_back(enc_grad, x_full, inv_rms, gain, w_down, w_up):
    flat_grad = enc_grad.reshape(-1, enc_grad.shape[-1])
    lat_grad = jnp.dot(flat_grad, w_up.T, preferred_element_type=jnp.float32).astype(jnp.bfloat16)
    hid_grad = jnp.dot(lat_grad, w_down.T, preferred_element_type=jnp.float32).reshape(x_full.shape)
    scaled = hid_grad * gain
    normed = x_full * inv_rms
    x_grad = enc_grad.astype(jnp.float32) + inv_rms * (
        scaled - normed * jnp.mean(scaled * normed, axis=-1, keepdims=True)
    )
    return jnp.sum(x_grad, axis=-2), lat_grad


def attend(query_rows, cot_rows, encoded, block_len, w_kv):
    token_count, head_cols = query_rows.shape
    block_count, slot_len, enc_width = encoded.shape
    span_count = token_count // SPAN
    key_count = block_count * slot_len // span_count
    scaling = HEAD ** (-0.5)
    key_value = jnp.dot(
        encoded.reshape(block_count * slot_len, enc_width), w_kv, preferred_element_type=jnp.float32
    ).astype(jnp.bfloat16)
    key_rows = key_value[:, :head_cols].reshape(span_count, key_count, HEADS, HEAD)
    value_rows = key_value[:, head_cols:].reshape(span_count, key_count, HEADS, HEAD)
    q_heads = query_rows.reshape(span_count, SPAN, HEADS, HEAD)
    out_grad = cot_rows.reshape(span_count, SPAN, HEADS, HEAD)
    usable = (jnp.arange(slot_len, dtype=jnp.int32)[None, :] < block_len[:, None]).reshape(
        span_count, 1, 1, key_count
    )
    scores = (
        jnp.einsum("cqhd,ckhd->chqk", q_heads, key_rows, preferred_element_type=jnp.float32)
        * scaling
    )
    scores = jnp.where(usable, scores, FLOOR)
    row_max = jnp.max(scores, axis=-1, keepdims=True)
    raised = jnp.exp(scores - row_max)
    probs = raised / jnp.sum(raised, axis=-1, keepdims=True)
    probs_b = probs.astype(jnp.bfloat16)
    attn_out = (
        jnp.einsum("chqk,ckhd->cqhd", probs_b, value_rows, preferred_element_type=jnp.float32)
        .astype(jnp.bfloat16)
        .reshape(token_count, head_cols)
    )
    d_probs = jnp.einsum(
        "cqhd,ckhd->chqk", out_grad, value_rows, preferred_element_type=jnp.float32
    )
    delta = jnp.sum(probs * d_probs, axis=-1, keepdims=True)
    d_scores = (probs * (d_probs - delta)).astype(jnp.bfloat16)
    q_grad = (
        (
            jnp.einsum("chqk,ckhd->cqhd", d_scores, key_rows, preferred_element_type=jnp.float32)
            * scaling
        )
        .astype(jnp.bfloat16)
        .reshape(token_count, head_cols)
    )
    key_grad = (
        jnp.einsum("chqk,cqhd->ckhd", d_scores, q_heads, preferred_element_type=jnp.float32)
        * scaling
    ).astype(jnp.bfloat16)
    value_grad = jnp.einsum(
        "chqk,cqhd->ckhd", probs_b, out_grad, preferred_element_type=jnp.float32
    ).astype(jnp.bfloat16)
    kv_grad = jnp.concatenate(
        [
            key_grad.reshape(block_count * slot_len, head_cols),
            value_grad.reshape(block_count * slot_len, head_cols),
        ],
        axis=1,
    )
    enc_grad = lax.dot_general(
        kv_grad, w_kv, (((1,), (1,)), ((), ())), preferred_element_type=jnp.float32
    ).astype(jnp.bfloat16)
    return (attn_out, q_grad, enc_grad.reshape(block_count, slot_len, enc_width))


def body(
    queries, cotangent, cond, nbr_owner, nbr_block, database, lengths, gain, w_down, w_up, w_kv
):
    pools = lax.axis_size("pool")
    columns = lax.axis_size("dp")
    relay_row = pools - 1
    pool_index = lax.axis_index("pool")
    me = lax.axis_index("dp")
    on_encoder = pool_index == relay_row
    span_count = cond.shape[2]
    enc_width = cond.shape[3]
    nbr_count = nbr_owner.shape[3]
    per_device = span_count * nbr_count
    blk_dev = database.shape[2]
    slot_len = database.shape[3]
    token_count = queries.shape[2]
    head_cols = queries.shape[3]
    quarter = slot_len // pools

    meta = jnp.concatenate([nbr_owner.reshape(-1), nbr_block.reshape(-1), lengths.reshape(-1)])
    meta = lax.all_gather(meta, ("pool", "dp"), axis=0).reshape(pools, columns, -1)
    owner = jnp.swapaxes(meta[:relay_row, :, :per_device], 0, 1).reshape(columns, -1)
    block = jnp.swapaxes(meta[:relay_row, :, per_device : 2 * per_device], 0, 1).reshape(
        columns, -1
    )
    lens = meta[relay_row, :, 2 * per_device :]

    db4 = database.reshape(blk_dev, pools, quarter, enc_width)
    db4 = jnp.swapaxes(db4, 0, 1)
    mine = lax.all_to_all(db4, "pool", split_axis=0, concat_axis=0, tiled=True)[relay_row]

    live = owner.shape[1]
    order = jnp.arange(live, dtype=jnp.int32)[None, :]
    named = owner == me
    first = jnp.min(jnp.where(named, order, live), axis=1, keepdims=True)
    last = jnp.max(jnp.where(named, order, -1), axis=1, keepdims=True)
    b0 = jnp.sum(jnp.where(order == first, block, 0), axis=1)
    b1 = jnp.sum(jnp.where(order == last, block, 0), axis=1)
    slot_block = jnp.stack([b0, b1], axis=1).reshape(-1)
    send = jnp.take(mine, slot_block, axis=0).reshape(columns, 2, quarter, enc_width)

    got = lax.all_to_all(send, "dp", split_axis=0, concat_axis=0, tiled=True)
    got = got.reshape(columns * 2, quarter, enc_width)

    my_owner = lax.dynamic_index_in_dim(owner, me, 0, keepdims=False)
    my_block = lax.dynamic_index_in_dim(block, me, 0, keepdims=False)
    earlier = jnp.tril(jnp.ones((live, live), jnp.int32), -1)
    later = jnp.max(
        jnp.where(my_owner[:, None] == my_owner[None, :], earlier, 0), axis=1
    )
    position = my_owner * 2 + later
    pick = jnp.take(got, position, axis=0).reshape(relay_row, per_device, quarter, enc_width)
    pick = jnp.concatenate([pick, pick[:1]], axis=0)
    blocks = lax.all_to_all(pick, "pool", split_axis=0, concat_axis=0, tiled=True)
    blocks = jnp.swapaxes(blocks, 0, 1).reshape(per_device, slot_len, enc_width)

    own_row = jnp.minimum(pool_index, relay_row - 1)
    dec_owner = lax.dynamic_slice_in_dim(my_owner, own_row * per_device, per_device, 0)
    dec_block = lax.dynamic_slice_in_dim(my_block, own_row * per_device, per_device, 0)
    my_len = jnp.take(lens.reshape(-1), dec_owner * blk_dev + dec_block)

    def run(query_rows, cot_rows, blocks, my_len, cond_rows):
        cond_rep = jnp.repeat(cond_rows, nbr_count, axis=0)
        encoded, x_full, inv_rms, hidden, latent = encode_rows(
            blocks, cond_rep, gain, w_down, w_up
        )
        attn_out, q_grad, enc_grad = attend(query_rows, cot_rows, encoded, my_len, w_kv)
        cond_grad, lat_grad = encode_back(enc_grad, x_full, inv_rms, gain, w_down, w_up)
        flat_grad = enc_grad.reshape(-1, enc_width)
        down = lax.dot_general(
            hidden, lat_grad, (((0,), (0,)), ((), ())), preferred_element_type=jnp.float32
        )
        up = lax.dot_general(
            flat_grad, latent, (((0,), (0,)), ((), ())), preferred_element_type=jnp.float32
        )
        cond_grad = jnp.sum(cond_grad.reshape(span_count, nbr_count, enc_width), axis=1)
        return attn_out, q_grad, cond_grad, jnp.concatenate([down, up], axis=1)

    def skip(query_rows, cot_rows, blocks, my_len, cond_rows):
        return (
            jnp.zeros((token_count, head_cols), jnp.bfloat16),
            jnp.zeros((token_count, head_cols), jnp.bfloat16),
            jnp.zeros((span_count, enc_width), jnp.float32),
            jnp.zeros((enc_width, 2 * w_down.shape[1]), jnp.float32),
        )

    attn_out, q_grad, cond_grad, adapter = lax.cond(
        on_encoder,
        skip,
        run,
        queries.reshape(token_count, head_cols),
        cotangent.reshape(token_count, head_cols),
        blocks,
        my_len,
        cond.reshape(span_count, enc_width),
    )
    adapter_grad = lax.psum_scatter(
        adapter, ("pool", "dp"), scatter_dimension=0, tiled=True
    )
    return (
        attn_out.reshape(1, 1, token_count, head_cols),
        q_grad.reshape(1, 1, token_count, head_cols),
        cond_grad.reshape(1, 1, span_count, enc_width),
        adapter_grad,
    )


def solution(mesh):
    return jax.shard_map(
        body,
        mesh=mesh,
        in_specs=(
            P("pool", "dp", None, None),
            P("pool", "dp", None, None),
            P("pool", "dp", None, None),
            P("pool", "dp", None, None),
            P("pool", "dp", None, None),
            P("pool", "dp", None, None, None),
            P("pool", "dp", None),
            P(),
            P(),
            P(),
            P(),
        ),
        out_specs=(
            P("pool", "dp", None, None),
            P("pool", "dp", None, None),
            P("pool", "dp", None, None),
            P(("pool", "dp"), None),
        ),
        check_vma=False,
    )
```

time: 757 us -> 379 us (0.50)
  waiting for transfers between devices: 475 us -> 187 us
  starting transfers between devices: 60.3 us -> 17 us
  local copies, waits for them, and re-layouts: 78.1 us -> 38.1 us
    all_to_all x6 -> x3, waiting for transfers between devices: 233 us -> 41.1 us  [the longest x1 26.2 us: body(): got = lax.all_to_all(send, 'dp', split_axis=0, concat_axis=0, tiled=True)]
    unnamed x0 -> x1, blocking collectives: none -> 83.7 us
    psum x1 -> x0, waiting for transfers between devices: 83.4 us -> none  [spread(): return lax.psum(block, axis)]
    psum x2 -> x0, blocking collectives: 55.8 us -> none  [spread(): return lax.psum(block, axis)]
    all_to_all x6 -> x3, starting transfers between devices: 59.7 us -> 17 us  [the longest x1 7.25 us: body(): lax.all_to_all(pick, 'pool', split_axis=0, concat_axis=0, tiled=True)]
    all_gather x1 -> x0, waiting for transfers between devices: 37.9 us -> none  [body(): up_grads = lax.all_gather(enc_grad[None], 'pool', axis=0, tiled=True)]
    unnamed x4 -> x2, waiting for transfers between devices: 121 us -> 146 us
    all_gather x3 -> x0, blocking collectives: 21.4 us -> none  [the longest x1 7.77 us: body(): lax.all_gather(nbr_owner.reshape(1, per_device), 'pool', axis=0, tiled=True)]
  transfers between devices with their start and end apart: 9 -> 4, of which waited for: 7 -> 3; matrix products, arithmetic and copies ran while one was open for 3% -> 1% of each run, Pallas kernels for 0% -> 0%
where the time goes in v1:
time: 379 us; the launch traced here: 378 us
  waiting for transfers between devices  187 us (49%)
  blocking collectives  83.7 us (22%)
  local copies, waits for them, and re-layouts  38.1 us (10%)
  matrix products  28.7 us (8%)
  starting transfers between devices  17 us (4%)
  between operations  14.2 us (4%)
  other arithmetic  9.03 us (2%)
    unnamed x2, waiting for transfers between devices  146 us
    unnamed x1, blocking collectives  83.7 us
    all_to_all x1, waiting for transfers between devices, body(): got = lax.all_to_all(send, 'dp', split_axis=0, concat_axis=0, tiled=True)  26.2 us
    all_to_all x1, waiting for transfers between devices, body(): lax.all_to_all(pick, 'pool', split_axis=0, concat_axis=0, tiled=True)  14.8 us
    cond x36, local copies, waits for them, and re-layouts  8.36 us
  transfers between devices with their start and end apart: 4, of which 3 were waited for; matrix products, arithmetic and copies ran while one was open for 1% of the time, Pallas kernels for 0%

profile of v1, /device:TPU:1, one launch (start us, length us, event | category | flops | bytes accessed | tf_op | source)
XLA Modules:
  0.0 378.4 jit_solution(11166723640282858294)
XLA Ops:
  7.2 3.2 copy.171
  10.4 5.8 %all-to-all-start = ((bf16[4,16,32,512]{3,2,1,0:T(8,128)(2,1)}), bf16[4,16,32,512]{3,2,1,0:T(8,128)(2,1)S(1)}, u32[]{:S(2)}, u32[]{:S(2)}) async-start(bf16[4,16,32,512]{3,2,1,0:T(8,128)(2,1)} %copy.171), calls=%async_computation | async-start | bytes 4194304 | tf_op jit(solution)/shard_map/all_to_all | solution.py:128
  16.7 83.7 %all-reduce = s32[4096]{0:T(1024)S(1)} all-reduce(s32[4096]{0:T(1024)S(1)} %add_dynamic-update-slice_fusion), channel_id=2, replica_groups=mesh['pool'=4,'dp'=32] {'pool','dp'}, use_global_device_ids=true, to_apply=%add | all-reduce | flops 4096 | bytes 32768
  102.0 1.6 broadcast_select_fusion
  103.6 4.0 %all-to-all-start.1 = ((bf16[32,2,32,512]{3,2,1,0:T(8,128)(2,1)}), bf16[32,2,32,512]{3,2,1,0:T(8,128)(2,1)S(1)}, u32[]{:S(2)}, u32[]{:S(2)}) async-start(bf16[32,2,32,512]{3,2,1,0:T(8,128)(2,1)} %broadcast_select_fusion), calls=%async_computation.1 | async-start | bytes 4194304 | tf_op jit(solution)/shard_map/all_to_all | solution.py:140
  108.4 26.2 %all-to-all-done.1 = bf16[32,2,32,512]{3,2,1,0:T(8,128)(2,1)S(1)} async-done(((bf16[32,2,32,512]{3,2,1,0:T(8,128)(2,1)}), bf16[32,2,32,512]{3,2,1,0:T(8,128)(2,1)S(1)}, u32[]{:S(2)}, u32[]{:S(2)}) %all-to-all-start.1) | async-done | bytes 2097184 | tf_op jit(solution)/shard_map/all_to_all | solution.py:140
  136.5 7.3 %all-to-all-start.2 = ((bf16[4,8,32,512]{3,2,1,0:T(8,128)(2,1)}), bf16[4,8,32,512]{3,2,1,0:T(8,128)(2,1)S(1)}, u32[]{:S(2)}, u32[]{:S(2)}) async-start(bf16[4,8,32,512]{3,2,1,0:T(8,128)(2,1)} %pad_maximum_fusion.1), calls=%async_computation.2 | async-start | bytes 2097152 | tf_op jit(solution)/shard_map/all_to_all | solution.py:152
  143.9 14.8 %all-to-all-done.2 = bf16[4,8,32,512]{3,2,1,0:T(8,128)(2,1)S(1)} async-done(((bf16[4,8,32,512]{3,2,1,0:T(8,128)(2,1)}), bf16[4,8,32,512]{3,2,1,0:T(8,128)(2,1)S(1)}, u32[]{:S(2)}, u32[]{:S(2)}) %all-to-all-start.2) | async-done | bytes 1048608 | tf_op jit(solution)/shard_map/all_to_all | solution.py:152
  158.8 64.3 %conditional.1 = (f32[512,512]{0,1:T(8,128)S(1)}, bf16[1,1,256,2048]{3,2,1,0:T(8,128)(2,1)}, bf16[1,1,256,2048]{3,2,1,0:T(8,128)(2,1)}, f32[1,1,4,512]{3,2,1,0:T(4,128)S(1)}) conditional(s32[]{:T(128)} %convert_element_type.105, (bf16[8,4,32,512]{3,2,0,1:T(8,128)(2,1)S(1)}, bf16[1,1,4,512]{3,2,1,0:T(4,128)(2,1)S(1)}, f32[512]{0:T(512)S(1)}, ...), branch_computations={%region_5.0_spmd.clone.clone, %region_13.14_spmd} | conditional | flops 11874335744 | bytes 366382048 | solution.py:185
  164.2 4.7 %convolution_convert_fusion = bf16[1024,4096]{1,0:T(8,128)(2,1)S(1)} fusion(bf16[1024,512]{1,0:T(8,128)(2,1)S(1)} %add_convert_fusion, bf16[512,4096]{1,0:T(8,128)(2,1)S(1)} %copy-done.21), kind=kOutput, calls=%fused_computation.9 | convolution fusion | flops 4299161600 | bytes 13631488 | tf_op jit(solution)/shard_map/cond/branch_0_fun/dot_general | solution.py:42
  174.9 1.8 fusion.57
  176.8 1.7 fusion.38
  178.7 1.7 copy.183
  180.4 2.3 reshape.386
  182.7 6.1 %fusion.6 = (f32[4,16,64]{2,1,0:T(8,128)S(1)}, f32[4,16,256,64]{2,3,1,0:T(8,128)S(1)}) fusion(f32[4,16,64,256]{3,2,1,0:T(8,128)} %copy-done.6, f32[4,16,64]{2,1,0:T(8,128)S(1)} %get-tuple-element.280, bf16[4,64,16,128]{3,2,1,0:T(8,128)(2,1)} %bitcast.197, bf16[4,256,16,128]{3,2,1,0:T(8,128)(2,1)} %bitcast.192), kind=kOutput, calls=%fused_computation.17 | convolution fusion | flops 271577088 | bytes 13664256 | tf_op jit(solution)/shard_map/cond/branch_0_fun/cqhd,ckhd->chqk/dot_general | solution.py:66
  193.0 2.7 convert_bitcast_fusion
  195.6 4.6 %copy.182 = bf16[4,256,16,128]{3,2,1,0:T(8,128)(2,1)} copy(bf16[4,256,16,128]{3,1,2,0:T(8,128)(2,1)S(1)} %convert_bitcast_fusion) | data formatting | bytes 8388608 | tf_op jit(solution)/shard_map/cond/branch_0_fun/convert_element_type | solution.py:85
  200.3 1.7 copy.184
  202.0 2.3 reshape.387
  204.2 3.2 fusion.5
  207.5 2.7 copy.181
  210.2 4.8 %copy_bitcast_fusion = (bf16[1024,2048]{1,0:T(8,128)(2,1)S(1)}, bf16[1024,2048]{1,0:T(8,128)(2,1)S(1)}) fusion(bf16[128,8,16,128]{3,2,1,0:T(8,128)(2,1)S(1)} %bitcast.185, bf16[128,8,16,128]{3,2,1,0:T(8,128)(2,1)S(1)} %bitcast.186), kind=kLoop, calls=%fused_computation.11 | loop fusion | bytes 16777216 | tf_op jit(solution)/shard_map/cond/branch_0_fun/reshape | solution.py:89
  215.0 4.5 %fusion.32 = bf16[1024,512]{1,0:T(8,128)(2,1)S(1)} fusion(bf16[512,4096]{1,0:T(8,128)(2,1)S(1)} %copy-done.22, bf16[1024,2048]{1,0:T(8,128)(2,1)S(1)} %get-tuple-element.286, bf16[1024,2048]{1,0:T(8,128)(2,1)S(1)} %get-tuple-element.287), kind=kOutput, calls=%fused_computation.52 | convolution fusion | flops 4312268800 | bytes 13631488 | tf_op jit(solution)/shard_map/cond/branch_0_fun/dot_general | solution.py:93
  224.5 145.7 %all-reduce.4.cloned.1.call-done = f32[512,512]{1,0:T(8,128)} async-done(((f32[512,512]{1,0:T(8,128)}), f32[512,512]{1,0:T(8,128)}) %all-reduce.4.cloned.1.call-update) | async-done | bytes 1048592
  (127 shorter events, 26.3 us)
Async XLA Ops:
  7.2 9.0 %copy-start.18 = (s32[1,1,4,2]{2,3,1,0:T(2,128)S(1)}, s32[1,1,4,2]{2,3,1,0:T(2,128)}, u32[]{:S(2)}) copy-start(s32[1,1,4,2]{2,3,1,0:T(2,128)} %param.16) | copy-start | bytes 100
  7.2 9.2 %copy-start.19 = (s32[1,1,4,2]{2,3,1,0:T(2,128)S(1)}, s32[1,1,4,2]{2,3,1,0:T(2,128)}, u32[]{:S(2)}) copy-start(s32[1,1,4,2]{2,3,1,0:T(2,128)} %param.17) | copy-start | bytes 100
  7.2 9.4 %copy-start.20 = (s32[1,1,16]{2,1,0:T(1,128)S(1)}, s32[1,1,16]{2,1,0:T(1,128)}, u32[]{:S(2)}) copy-start(s32[1,1,16]{2,1,0:T(1,128)} %param.19) | copy-start | bytes 196
  10.4 90.8 %all-to-all-start = ((bf16[4,16,32,512]{3,2,1,0:T(8,128)(2,1)}), bf16[4,16,32,512]{3,2,1,0:T(8,128)(2,1)S(1)}, u32[]{:S(2)}, u32[]{:S(2)}) async-start(bf16[4,16,32,512]{3,2,1,0:T(8,128)(2,1)} %copy.171), calls=%async_computation | async-start | bytes 4194304 | tf_op jit(solution)/shard_map/all_to_all | solution.py:128
  103.6 31.0 %all-to-all-start.1 = ((bf16[32,2,32,512]{3,2,1,0:T(8,128)(2,1)}), bf16[32,2,32,512]{3,2,1,0:T(8,128)(2,1)S(1)}, u32[]{:S(2)}, u32[]{:S(2)}) async-start(bf16[32,2,32,512]{3,2,1,0:T(8,128)(2,1)} %broadcast_select_fusion), calls=%async_computation.1 | async-start | bytes 4194304 | tf_op jit(solution)/shard_map/all_to_all | solution.py:140
  107.6 51.2 %copy-start.9 = (bf16[512,256]{1,0:T(8,128)(2,1)S(1)}, bf16[512,256]{1,0:T(8,128)(2,1)}, u32[]{:S(2)}) copy-start(bf16[512,256]{1,0:T(8,128)(2,1)} %param.21) | copy-start | bytes 786436
  107.6 51.2 %copy-start.15 = (f32[512]{0:T(512)S(1)}, f32[512]{0:T(512)}, u32[]{:S(2)}) copy-start(f32[512]{0:T(512)} %param.20) | copy-start | bytes 6148
  107.6 51.2 %copy-start.17 = (bf16[1,1,4,512]{3,2,1,0:T(4,128)(2,1)S(1)}, bf16[1,1,4,512]{3,2,1,0:T(4,128)(2,1)}, u32[]{:S(2)}) copy-start(bf16[1,1,4,512]{3,2,1,0:T(4,128)(2,1)} %param.15) | copy-start | bytes 12292
  135.2 23.6 %copy-start.11 = (bf16[1,1,256,2048]{3,2,1,0:T(8,128)(2,1)S(1)}, bf16[1,1,256,2048]{3,2,1,0:T(8,128)(2,1)}, u32[]{:S(2)}) copy-start(bf16[1,1,256,2048]{3,2,1,0:T(8,128)(2,1)} %param.14) | copy-start | bytes 3145732
  136.5 22.2 %all-to-all-start.2 = ((bf16[4,8,32,512]{3,2,1,0:T(8,128)(2,1)}), bf16[4,8,32,512]{3,2,1,0:T(8,128)(2,1)S(1)}, u32[]{:S(2)}, u32[]{:S(2)}) async-start(bf16[4,8,32,512]{3,2,1,0:T(8,128)(2,1)} %pad_maximum_fusion.1), calls=%async_computation.2 | async-start | bytes 2097152 | tf_op jit(solution)/shard_map/all_to_all | solution.py:152
  143.8 226.4 %all-reduce.4.cloned.1.call-start = ((), (), s32[]{:S(2)}) async-start(), calls=%async_computation.3 | async-start | bytes 2097152
  160.5 2.1 copy-start.10
  160.9 2.0 copy-start.13
  161.4 2.9 copy-start.21
  171.6 5.2 %copy-start.8 = (bf16[128,8,16,128]{3,2,1,0:T(8,128)(2,1)}, bf16[128,8,16,128]{3,2,1,0:T(8,128)(2,1)S(1)}, u32[]{:S(2)}) copy-start(bf16[128,8,16,128]{3,2,1,0:T(8,128)(2,1)S(1)} %copy.192) | copy-start | bytes 12582916 | tf_op jit(solution)/shard_map/cond
  173.0 1.9 copy-start
  176.7 2.0 copy-start.6
  182.7 6.1 %copy-start.7 = (f32[4,16,64,256]{3,2,1,0:T(8,128)S(1)}, f32[4,16,64,256]{3,2,1,0:T(8,128)}, u32[]{:S(2)}) copy-start(f32[4,16,64,256]{3,2,1,0:T(8,128)} %copy-done.6) | copy-start | bytes 12582916 | tf_op jit(solution)/shard_map/cond
  188.8 2.8 copy-start.1
  207.4 2.7 copy-start.2
  210.2 4.8 %copy-start.22 = (bf16[512,4096]{1,0:T(8,128)(2,1)S(1)}, bf16[512,4096]{1,0:T(8,128)(2,1)}, u32[]{:S(2)}) copy-start(bf16[512,4096]{1,0:T(8,128)(2,1)} %get-tuple-element.255) | copy-start | bytes 12582916 | tf_op jit(solution)/shard_map/cond
  215.0 4.5 %copy-start.5 = (bf16[1024,256]{1,0:T(8,128)(2,1)S(1)}, bf16[1024,256]{1,0:T(8,128)(2,1)}, u32[]{:S(2)}) copy-start(bf16[1024,256]{1,0:T(8,128)(2,1)} %copy-done.4) | copy-start | bytes 1572868 | tf_op jit(solution)/shard_map/cond
  215.0 5.0 %copy-start.14 = (bf16[256,512]{1,0:T(8,128)(2,1)S(1)}, bf16[256,512]{1,0:T(8,128)(2,1)}, u32[]{:S(2)}) copy-start(bf16[256,512]{1,0:T(8,128)(2,1)} %get-tuple-element.254) | copy-start | bytes 786436 | tf_op jit(solution)/shard_map/cond
  223.1 148.4 %copy-start.16 = (f32[1,1,4,512]{3,2,1,0:T(4,128)}, f32[1,1,4,512]{3,2,1,0:T(4,128)S(1)}, u32[]{:S(2)}) copy-start(f32[1,1,4,512]{3,2,1,0:T(4,128)S(1)} %get-tuple-element.104) | copy-start | bytes 24580
  (3 other events, 4.3 us)
Sparse Core Ops, SparseCore 0:
  224.6 145.5 all-reduce.3

commit v2 on v1

v2 whole, which is shorter than its diff:
```python
import functools
import jax
import jax.numpy as jnp
from jax import lax
from jax.experimental import pallas as pl
from jax.experimental.pallas import tpu as pltpu
from jax.sharding import PartitionSpec as P

HEAD = 128
SPAN = 64
EPSILON = 1e-06
FLOOR = -1e30
F32 = jnp.float32
BF16 = jnp.bfloat16


def dot_nn(a, b):
    return lax.dot_general(a, b, (((1,), (0,)), ((), ())), preferred_element_type=F32)


def dot_nt(a, b):
    return lax.dot_general(a, b, (((1,), (1,)), ((), ())), preferred_element_type=F32)


def dot_tn(a, b):
    return lax.dot_general(a, b, (((0,), (0,)), ((), ())), preferred_element_type=F32)


def attend_kernel(
    unroll, info, q_ref, do_ref, blk_ref, cond_ref, gain_ref, wd_ref, wu_ref, wkv_ref,
    out_ref, dq_ref, cg_ref, ad_ref, kv, kvg,
):
    c = pl.program_id(0)
    pools, nbr, quarter, width = blk_ref.shape
    slot_len = pools * quarter
    keys = nbr * slot_len
    hq = q_ref.shape[1]
    rank = wd_ref.shape[1]
    scaling = HEAD ** (-0.5)
    per_device = pl.num_programs(0) * nbr
    on_encoder = info[per_device] == 1

    @pl.when(c == 0)
    def _():
        ad_ref[...] = jnp.zeros_like(ad_ref)
        cg_ref[...] = jnp.zeros_like(cg_ref)

    @pl.when(on_encoder)
    def _():
        out_ref[...] = jnp.zeros_like(out_ref)
        dq_ref[...] = jnp.zeros_like(dq_ref)

    @pl.when(jnp.logical_not(on_encoder))
    def _():
        rows = jnp.concatenate(
            [blk_ref[p, n] for n in range(nbr) for p in range(pools)], axis=0
        ).astype(F32)
        cond = cond_ref[...].astype(F32)
        pick = lax.broadcasted_iota(jnp.int32, cond.shape, 0) == c
        cond_row = jnp.sum(jnp.where(pick, cond, 0.0), axis=0, keepdims=True)
        gain = gain_ref[...]
        x_full = rows + cond_row
        inv_rms = lax.rsqrt(jnp.mean(x_full * x_full, axis=-1, keepdims=True) + EPSILON)
        normed = x_full * inv_rms
        hidden = (normed * gain).astype(BF16)
        latent = dot_nn(hidden, wd_ref[...]).astype(BF16)
        encoded = (x_full + dot_nn(latent, wu_ref[...])).astype(BF16)
        for t in range(2 * hq // 512):
            cols = pl.ds(t * 512, 512)
            kv[:, cols] = dot_nn(encoded, wkv_ref[:, cols]).astype(BF16)

        slot = lax.broadcasted_iota(jnp.int32, (SPAN, keys), 1)
        bound = jnp.where(slot < slot_len, info[c * nbr], info[c * nbr + 1] + slot_len)
        usable = slot < bound

        def head(h):
            qs = pl.ds(pl.multiple_of(h * HEAD, HEAD), HEAD)
            vs = pl.ds(pl.multiple_of(hq + h * HEAD, HEAD), HEAD)
            q = q_ref[:, qs]
            do = do_ref[:, qs]
            k = kv[:, qs]
            v = kv[:, vs]
            s = jnp.where(usable, dot_nt(q, k) * scaling, FLOOR)
            dp = dot_nt(do, v)
            e = jnp.exp(s - jnp.max(s, axis=-1, keepdims=True))
            p = e * (1.0 / jnp.sum(e, axis=-1, keepdims=True))
            pb = p.astype(BF16)
            pdp = p * dp
            delta = jnp.sum(pdp, axis=-1, keepdims=True)
            ds = (pdp - p * delta).astype(BF16)
            out_ref[:, qs] = dot_nn(pb, v).astype(BF16)
            dq_ref[:, qs] = (dot_nn(ds, k) * scaling).astype(BF16)
            kvg[:, qs] = (dot_tn(ds, q) * scaling).astype(BF16)
            kvg[:, vs] = dot_tn(pb, do).astype(BF16)

        def heads(i, carry):
            for u in range(unroll):
                head(i * unroll + u)
            return carry

        lax.fori_loop(0, hq // HEAD // unroll, heads, 0)

        enc_grad = dot_nt(kvg[...], wkv_ref[...]).astype(BF16)
        lat_grad = dot_nt(enc_grad, wu_ref[...]).astype(BF16)
        scaled = dot_nt(lat_grad, wd_ref[...]) * gain
        mean = jnp.mean(scaled * normed, axis=-1, keepdims=True)
        x_grad = enc_grad.astype(F32) + inv_rms * (scaled - normed * mean)
        cg_ref[pl.ds(c, 1), :] = jnp.sum(x_grad, axis=0, keepdims=True)
        ad_ref[:, :rank] += dot_tn(hidden, lat_grad)
        ad_ref[:, rank:] += dot_tn(enc_grad, latent)


def attend(info, queries, cotangent, blocks, cond, gain, w_down, w_up, w_kv, unroll=2):
    tokens, hq = queries.shape
    pools, per_device, quarter, width = blocks.shape
    spans = cond.shape[0]
    nbr = per_device // spans
    rank = w_down.shape[1]
    whole = lambda shape: pl.BlockSpec(shape, lambda c, info: (0,) * len(shape))
    rows = pl.BlockSpec((SPAN, hq), lambda c, info: (c, 0))
    return pl.pallas_call(
        functools.partial(attend_kernel, unroll),
        out_shape=(
            jax.ShapeDtypeStruct((tokens, hq), BF16),
            jax.ShapeDtypeStruct((tokens, hq), BF16),
            jax.ShapeDtypeStruct((spans, width), F32),
            jax.ShapeDtypeStruct((width, 2 * rank), F32),
        ),
        grid_spec=pltpu.PrefetchScalarGridSpec(
            num_scalar_prefetch=1,
            grid=(spans,),
            in_specs=[
                rows,
                rows,
                pl.BlockSpec((pools, nbr, quarter, width), lambda c, info: (0, c, 0, 0)),
                whole((spans, width)),
                whole((1, width)),
                whole((width, rank)),
                whole((rank, width)),
                whole((width, 2 * hq)),
            ],
            out_specs=[rows, rows, whole((spans, width)), whole((width, 2 * rank))],
            scratch_shapes=[
                pltpu.VMEM((nbr * pools * quarter, 2 * hq), BF16),
                pltpu.VMEM((nbr * pools * quarter, 2 * hq), BF16),
            ],
        ),
        compiler_params=pltpu.CompilerParams(
            dimension_semantics=("arbitrary",), vmem_limit_bytes=56 << 20
        ),
        name="attend",
    )(info, queries, cotangent, blocks, cond, gain.reshape(1, width), w_down, w_up, w_kv)


def body(
    queries, cotangent, cond, nbr_owner, nbr_block, database, lengths, gain, w_down, w_up, w_kv
):
    pools = lax.axis_size("pool")
    columns = lax.axis_size("dp")
    relay_row = pools - 1
    pool_index = lax.axis_index("pool")
    me = lax.axis_index("dp")
    on_encoder = pool_index == relay_row
    span_count = cond.shape[2]
    enc_width = cond.shape[3]
    nbr_count = nbr_owner.shape[3]
    per_device = span_count * nbr_count
    blk_dev = database.shape[2]
    slot_len = database.shape[3]
    token_count = queries.shape[2]
    head_cols = queries.shape[3]
    quarter = slot_len // pools

    meta = jnp.concatenate([nbr_owner.reshape(-1), nbr_block.reshape(-1), lengths.reshape(-1)])
    meta = jnp.broadcast_to(meta[None], (pools * columns,) + meta.shape)
    meta = lax.all_to_all(meta, ("pool", "dp"), split_axis=0, concat_axis=0, tiled=True)
    meta = meta.reshape(pools, columns, -1)
    owner = jnp.swapaxes(meta[:relay_row, :, :per_device], 0, 1).reshape(columns, -1)
    block = jnp.swapaxes(meta[:relay_row, :, per_device : 2 * per_device], 0, 1).reshape(
        columns, -1
    )
    lens = meta[relay_row, :, 2 * per_device :]

    db4 = database.reshape(blk_dev, pools, quarter, enc_width)
    db4 = jnp.swapaxes(db4, 0, 1)
    mine = lax.all_to_all(db4, "pool", split_axis=0, concat_axis=0, tiled=True)[relay_row]

    live = owner.shape[1]
    order = jnp.arange(live, dtype=jnp.int32)[None, :]
    named = owner == me
    first = jnp.min(jnp.where(named, order, live), axis=1, keepdims=True)
    last = jnp.max(jnp.where(named, order, -1), axis=1, keepdims=True)
    b0 = jnp.sum(jnp.where(order == first, block, 0), axis=1)
    b1 = jnp.sum(jnp.where(order == last, block, 0), axis=1)
    slot_block = jnp.stack([b0, b1], axis=1).reshape(-1)
    send = jnp.take(mine, slot_block, axis=0).reshape(columns, 2, quarter, enc_width)

    got = lax.all_to_all(send, "dp", split_axis=0, concat_axis=0, tiled=True)
    got = got.reshape(columns * 2, quarter, enc_width)

    my_owner = lax.dynamic_index_in_dim(owner, me, 0, keepdims=False)
    my_block = lax.dynamic_index_in_dim(block, me, 0, keepdims=False)
    earlier = jnp.tril(jnp.ones((live, live), jnp.int32), -1)
    later = jnp.max(
        jnp.where(my_owner[:, None] == my_owner[None, :], earlier, 0), axis=1
    )
    position = my_owner * 2 + later
    pick = jnp.take(got, position, axis=0).reshape(relay_row, per_device, quarter, enc_width)
    pick = jnp.concatenate([pick, pick[:1]], axis=0)
    blocks = lax.all_to_all(pick, "pool", split_axis=0, concat_axis=0, tiled=True)

    own_row = jnp.minimum(pool_index, relay_row - 1)
    dec_owner = lax.dynamic_slice_in_dim(my_owner, own_row * per_device, per_device, 0)
    dec_block = lax.dynamic_slice_in_dim(my_block, own_row * per_device, per_device, 0)
    my_len = jnp.take(lens.reshape(-1), dec_owner * blk_dev + dec_block)

    info = jnp.concatenate([my_len, on_encoder.astype(jnp.int32)[None]])
    attn_out, q_grad, cond_grad, adapter = attend(
        info,
        queries.reshape(token_count, head_cols),
        cotangent.reshape(token_count, head_cols),
        blocks,
        cond.reshape(span_count, enc_width),
        gain,
        w_down,
        w_up,
        w_kv,
        unroll=4,
    )
    parts = pools * columns
    adapter = adapter.reshape(parts, enc_width // parts, -1)
    adapter = lax.all_to_all(adapter, ("pool", "dp"), split_axis=0, concat_axis=0, tiled=True)
    adapter_grad = jnp.sum(adapter, axis=0)
    return (
        attn_out.reshape(1, 1, token_count, head_cols),
        q_grad.reshape(1, 1, token_count, head_cols),
        cond_grad.reshape(1, 1, span_count, enc_width),
        adapter_grad,
    )


def solution(mesh):
    return jax.shard_map(
        body,
        mesh=mesh,
        in_specs=(
            P("pool", "dp", None, None),
            P("pool", "dp", None, None),
            P("pool", "dp", None, None),
            P("pool", "dp", None, None),
            P("pool", "dp", None, None),
            P("pool", "dp", None, None, None),
            P("pool", "dp", None),
            P(),
            P(),
            P(),
            P(),
        ),
        out_specs=(
            P("pool", "dp", None, None),
            P("pool", "dp", None, None),
            P("pool", "dp", None, None),
            P(("pool", "dp"), None),
        ),
        check_vma=False,
    )
```

time: 379 us -> 192 us (0.51)
  waiting for transfers between devices: 187 us -> 71.8 us
  blocking collectives: 83.7 us -> 24.4 us
  Pallas kernels: 0 us -> 50.9 us
  matrix products: 28.7 us -> 0 us
  local copies, waits for them, and re-layouts: 38.1 us -> 10.9 us
  between operations: 14.2 us -> 0.79 us
  starting transfers between devices: 17 us -> 26.8 us
    unnamed x2 -> x0, waiting for transfers between devices: 146 us -> none
    unnamed x1 -> x0, blocking collectives: 83.7 us -> none
    pallas_call x0 -> x1, Pallas kernels: none -> 50.9 us  [attend(): pl.pallas_call(functools.partial(attend_kernel, unroll), out_shape=(jax.S...]
    dot_general x14 -> x0, matrix products: 28.7 us -> none  [the longest x1 6.07 us: attend(): jnp.einsum('cqhd,ckhd->chqk', out_grad, value_rows, preferred_element_typ...]
    all_to_all x1, waiting for transfers between devices: 0.01 us -> 25.4 us  [body(): lax.all_to_all(db4, 'pool', split_axis=0, concat_axis=0, tiled=True)]
    all_to_all x0 -> x1, blocking collectives: none -> 24.4 us  [body(): lax.all_to_all(adapter, ('pool', 'dp'), split_axis=0, concat_axis=0, tile...]
    all_to_all x0 -> x1, starting transfers between devices: none -> 11.5 us  [body(): lax.all_to_all(meta, ('pool', 'dp'), split_axis=0, concat_axis=0, tiled=T...]
    convert_element_type x5 -> x0, local copies, waits for them, and re-layouts: 10.8 us -> none  [the longest x1 4.63 us: attend(): value_grad = jnp.einsum('chqk,cqhd->ckhd', probs_b, out_grad, preferred_e...]
  transfers between devices with their start and end apart: 4 -> 4, of which waited for: 3 -> 4; matrix products, arithmetic and copies ran while one was open for 1% -> 3% of each run, Pallas kernels for 0% -> 0%
where the time goes in v2:
time: 192 us; the launch traced here: 191 us
  waiting for transfers between devices  71.8 us (37%)
  Pallas kernels  50.9 us (27%)
  starting transfers between devices  26.8 us (14%)
  blocking collectives  24.4 us (13%)
  local copies, waits for them, and re-layouts  10.9 us (6%)
  other arithmetic  5.89 us (3%)
    pallas_call x1, Pallas kernels, attend(): pl.pallas_call(functools.partial(attend_kernel, unroll), out_shape=(jax.S...  50.9 us
    all_to_all x1, waiting for transfers between devices, body(): got = lax.all_to_all(send, 'dp', split_axis=0, concat_axis=0, tiled=True)  26.5 us
    all_to_all x1, waiting for transfers between devices, body(): lax.all_to_all(db4, 'pool', split_axis=0, concat_axis=0, tiled=True)  25.4 us
    all_to_all x1, blocking collectives, body(): lax.all_to_all(adapter, ('pool', 'dp'), split_axis=0, concat_axis=0, tile...  24.4 us
    all_to_all x1, waiting for transfers between devices, body(): lax.all_to_all(pick, 'pool', split_axis=0, concat_axis=0, tiled=True)  13.3 us
    all_to_all x1, starting transfers between devices, body(): lax.all_to_all(meta, ('pool', 'dp'), split_axis=0, concat_axis=0, tiled=T...  11.5 us
    all_to_all x1, starting transfers between devices, body(): lax.all_to_all(pick, 'pool', split_axis=0, concat_axis=0, tiled=True)  7.16 us
    all_to_all x1, waiting for transfers between devices, body(): lax.all_to_all(meta, ('pool', 'dp'), split_axis=0, concat_axis=0, tiled=T...  6.51 us
  transfers between devices with their start and end apart: 4, of which 4 were waited for; matrix products, arithmetic and copies ran while one was open for 3% of the time, Pallas kernels for 0%

profile of v2, /device:TPU:1, one launch (start us, length us, event | category | flops | bytes accessed | tf_op | source)
XLA Modules:
  0.0 191.5 jit_solution(8289408883461233027)
XLA Ops:
  0.6 0.8 copy.50
  1.5 0.8 copy.51
  2.3 0.7 pad_add_fusion.1
  3.1 0.7 broadcast_in_dim.73
  3.7 11.5 %all-to-all-start = ((s32[128,1,32]{2,1,0:T(1,128)}), s32[128,1,32]{2,1,0:T(1,128)S(1)}, u32[]{:S(2)}, u32[]{:S(2)}) async-start(s32[128,1,32]{2,1,0:T(1,128)} %broadcast_in_dim.73), calls=%async_computation | async-start | bytes 131072 | tf_op jit(solution)/shard_map/all_to_all | solution.py:176
  15.2 3.2 %copy.57 = bf16[4,16,32,512]{3,2,1,0:T(8,128)(2,1)} copy(bf16[4,16,32,512]{3,2,0,1:T(8,128)(2,1)} %bitcast.49) | data formatting | bytes 4194304 | tf_op jit(solution)/shard_map/transpose | solution.py:185
  18.4 6.5 %all-to-all-done = s32[128,1,32]{2,1,0:T(1,128)S(1)} async-done(((s32[128,1,32]{2,1,0:T(1,128)}), s32[128,1,32]{2,1,0:T(1,128)S(1)}, u32[]{:S(2)}, u32[]{:S(2)}) %all-to-all-start) | async-done | bytes 16416 | tf_op jit(solution)/shard_map/all_to_all | solution.py:176
  24.9 4.2 %all-to-all-start.1 = ((bf16[4,16,32,512]{3,2,1,0:T(8,128)(2,1)}), bf16[4,16,32,512]{3,2,1,0:T(8,128)(2,1)S(1)}, u32[]{:S(2)}, u32[]{:S(2)}) async-start(bf16[4,16,32,512]{3,2,1,0:T(8,128)(2,1)} %copy.57), calls=%async_computation.1 | async-start | bytes 4194304 | tf_op jit(solution)/shard_map/all_to_all | solution.py:186
  29.9 25.4 %all-to-all-done.1 = bf16[4,16,32,512]{3,2,1,0:T(8,128)(2,1)S(1)} async-done(((bf16[4,16,32,512]{3,2,1,0:T(8,128)(2,1)}), bf16[4,16,32,512]{3,2,1,0:T(8,128)(2,1)S(1)}, u32[]{:S(2)}, u32[]{:S(2)}) %all-to-all-start.1) | async-done | bytes 2097184 | tf_op jit(solution)/shard_map/all_to_all | solution.py:186
  55.3 0.7 gather_fusion.1
  56.0 1.6 broadcast_select_fusion
  57.6 4.0 %all-to-all-start.2 = ((bf16[32,2,32,512]{3,2,1,0:T(8,128)(2,1)}), bf16[32,2,32,512]{3,2,1,0:T(8,128)(2,1)S(1)}, u32[]{:S(2)}, u32[]{:S(2)}) async-start(bf16[32,2,32,512]{3,2,1,0:T(8,128)(2,1)} %broadcast_select_fusion), calls=%async_computation.2 | async-start | bytes 4194304 | tf_op jit(solution)/shard_map/all_to_all | solution.py:198
  62.3 26.5 %all-to-all-done.2 = bf16[32,2,32,512]{3,2,1,0:T(8,128)(2,1)S(1)} async-done(((bf16[32,2,32,512]{3,2,1,0:T(8,128)(2,1)}), bf16[32,2,32,512]{3,2,1,0:T(8,128)(2,1)S(1)}, u32[]{:S(2)}, u32[]{:S(2)}) %all-to-all-start.2) | async-done | bytes 2097184 | tf_op jit(solution)/shard_map/all_to_all | solution.py:198
  88.8 0.6 gather_fusion.2
  89.6 1.1 pad_maximum_fusion
  90.7 7.2 %all-to-all-start.3 = ((bf16[4,8,32,512]{3,2,1,0:T(8,128)(2,1)}), bf16[4,8,32,512]{3,2,1,0:T(8,128)(2,1)S(1)}, u32[]{:S(2)}, u32[]{:S(2)}) async-start(bf16[4,8,32,512]{3,2,1,0:T(8,128)(2,1)} %pad_maximum_fusion), calls=%async_computation.3 | async-start | bytes 2097152 | tf_op jit(solution)/shard_map/all_to_all | solution.py:210
  98.2 0.6 gather_fusion
  98.9 0.6 pad_add_fusion.2.info
  99.5 13.3 %all-to-all-done.3.blk_ref = bf16[4,8,32,512]{3,2,1,0:T(8,128)(2,1)S(1)} async-done(((bf16[4,8,32,512]{3,2,1,0:T(8,128)(2,1)}), bf16[4,8,32,512]{3,2,1,0:T(8,128)(2,1)S(1)}, u32[]{:S(2)}, u32[]{:S(2)}) %all-to-all-start.3) | async-done | bytes 1048608 | tf_op jit(solution)/shard_map/all_to_all | solution.py:210
  112.8 1.0 copy-done
  113.8 50.9 %attend.1 = (bf16[256,2048]{1,0:T(8,128)(2,1)}, bf16[256,2048]{1,0:T(8,128)(2,1)}, f32[4,512]{1,0:T(4,128)}, f32[512,512]{1,0:T(8,128)}) custom-call(s32[9]{0:T(128)} %pad_add_fusion.2.info, bf16[256,2048]{1,0:T(8,128)(2,1)} %bitcast.50, bf16[256,2048]{1,0:T(8,128)(2,1)} %bitcast.51, bf16[4,8,32,512]{3,2,1,0:T(8,128)(2,1)} %copy-done, ...), custom_call_target="tpu_custom_call" | custom-call | tf_op jit(solution)/shard_map/attend/pallas_call | solution.py:121
  164.7 1.5 reshape.239
  166.2 24.4 %all_to_all.26 = f32[128,4,512]{2,1,0:T(4,128)S(1)} all-to-all(f32[128,4,512]{2,1,0:T(4,128)S(1)} %reshape.239), channel_id=1, replica_groups=mesh['pool'=4,'dp'=32] {'pool','dp'}, dimensions={0} | all-to-all | bytes 2097152 | tf_op jit(solution)/shard_map/all_to_all | solution.py:232
  190.7 0.8 reduce_sum.29
  (35 shorter events, 2.2 us)
Async XLA Ops:
  3.7 21.2 %all-to-all-start = ((s32[128,1,32]{2,1,0:T(1,128)}), s32[128,1,32]{2,1,0:T(1,128)S(1)}, u32[]{:S(2)}, u32[]{:S(2)}) async-start(s32[128,1,32]{2,1,0:T(1,128)} %broadcast_in_dim.73), calls=%async_computation | async-start | bytes 131072 | tf_op jit(solution)/shard_map/all_to_all | solution.py:176
  24.9 30.4 %all-to-all-start.1 = ((bf16[4,16,32,512]{3,2,1,0:T(8,128)(2,1)}), bf16[4,16,32,512]{3,2,1,0:T(8,128)(2,1)S(1)}, u32[]{:S(2)}, u32[]{:S(2)}) async-start(bf16[4,16,32,512]{3,2,1,0:T(8,128)(2,1)} %copy.57), calls=%async_computation.1 | async-start | bytes 4194304 | tf_op jit(solution)/shard_map/all_to_all | solution.py:186
  57.6 31.1 %all-to-all-start.2 = ((bf16[32,2,32,512]{3,2,1,0:T(8,128)(2,1)}), bf16[32,2,32,512]{3,2,1,0:T(8,128)(2,1)S(1)}, u32[]{:S(2)}, u32[]{:S(2)}) async-start(bf16[32,2,32,512]{3,2,1,0:T(8,128)(2,1)} %broadcast_select_fusion), calls=%async_computation.2 | async-start | bytes 4194304 | tf_op jit(solution)/shard_map/all_to_all | solution.py:198
  90.7 22.1 %all-to-all-start.3 = ((bf16[4,8,32,512]{3,2,1,0:T(8,128)(2,1)}), bf16[4,8,32,512]{3,2,1,0:T(8,128)(2,1)S(1)}, u32[]{:S(2)}, u32[]{:S(2)}) async-start(bf16[4,8,32,512]{3,2,1,0:T(8,128)(2,1)} %pad_maximum_fusion), calls=%async_computation.3 | async-start | bytes 2097152 | tf_op jit(solution)/shard_map/all_to_all | solution.py:210
  112.8 1.0 copy-start

commit v3 on v2

--- a/solution.py
+++ b/solution.py
@@ -28,7 +28,7 @@
 
 def attend_kernel(
     unroll, info, q_ref, do_ref, blk_ref, cond_ref, gain_ref, wd_ref, wu_ref, wkv_ref,
-    out_ref, dq_ref, cg_ref, ad_ref, kv, kvg,
+    out_ref, dq_ref, cg_ref, part_ref, kv, kvg, ad_ref,
 ):
     c = pl.program_id(0)
     pools, nbr, quarter, width = blk_ref.shape
@@ -109,8 +109,15 @@
         ad_ref[:, :rank] += dot_tn(hidden, lat_grad)
         ad_ref[:, rank:] += dot_tn(enc_grad, latent)
 
-
-def attend(info, queries, cotangent, blocks, cond, gain, w_down, w_up, w_kv, unroll=2):
+    @pl.when(c == pl.num_programs(0) - 1)
+    def _():
+        columns, pools_out, piece, _ = part_ref.shape
+        for p in range(pools_out):
+            for j in range(columns):
+                part_ref[j, p] = ad_ref[pl.ds((p * columns + j) * piece, piece), :]
+
+
+def attend(columns, info, queries, cotangent, blocks, cond, gain, w_down, w_up, w_kv, unroll=2):
     tokens, hq = queries.shape
     pools, per_device, quarter, width = blocks.shape
     spans = cond.shape[0]
@@ -124,7 +131,7 @@
             jax.ShapeDtypeStruct((tokens, hq), BF16),
             jax.ShapeDtypeStruct((tokens, hq), BF16),
             jax.ShapeDtypeStruct((spans, width), F32),
-            jax.ShapeDtypeStruct((width, 2 * rank), F32),
+            jax.ShapeDtypeStruct((columns, pools, width // (pools * columns), 2 * rank), F32),
         ),
         grid_spec=pltpu.PrefetchScalarGridSpec(
             num_scalar_prefetch=1,
@@ -139,10 +146,16 @@
                 whole((rank, width)),
                 whole((width, 2 * hq)),
             ],
-            out_specs=[rows, rows, whole((spans, width)), whole((width, 2 * rank))],
+            out_specs=[
+                rows,
+                rows,
+                whole((spans, width)),
+                whole((columns, pools, width // (pools * columns), 2 * rank)),
+            ],
             scratch_shapes=[
                 pltpu.VMEM((nbr * pools * quarter, 2 * hq), BF16),
                 pltpu.VMEM((nbr * pools * quarter, 2 * hq), BF16),
+                pltpu.VMEM((width, 2 * rank), F32),
             ],
         ),
         compiler_params=pltpu.CompilerParams(
@@ -150,6 +163,374 @@
         ),
         name="attend",
     )(info, queries, cotangent, blocks, cond, gain.reshape(1, width), w_down, w_up, w_kv)
+
+
+MESH = pl.DeviceIdType.MESH
+
+
+def greet(pools, columns):
+    pool, me = lax.axis_index("pool"), lax.axis_index("dp")
+    barrier = pltpu.get_barrier_semaphore()
+
+    def hello(d, carry):
+        pl.semaphore_signal(
+            barrier, inc=1, device_id={"dp": lax.rem(me + d, columns)}, device_id_type=MESH
+        )
+        return carry
+
+    lax.fori_loop(1, columns, hello, 0)
+    for d in range(1, pools):
+        pl.semaphore_signal(
+            barrier, inc=1, device_id={"pool": lax.rem(pool + d, pools)}, device_id_type=MESH
+        )
+    pl.semaphore_wait(barrier, columns - 1 + pools - 1)
+
+
+def fetch_kernel(
+    pools, columns, owner_ref, block_ref, len_ref, db_ref, out_ref, info_ref,
+    row, metas, smeta, table, place, share, send, got, pick,
+    local_sem, base_send, base_recv, row_send, row_recv, meta_send, meta_recv,
+    slot_send, slot_recv, pick_send, pick_recv,
+):
+    pool, me = lax.axis_index("pool"), lax.axis_index("dp")
+    top = pools - 1
+    spans, nbr = owner_ref.shape
+    per = spans * nbr
+    blocks, quarter = share.shape[0], share.shape[1]
+    is_enc = pool == top
+    greet(pools, columns)
+
+    def base_copy(p):
+        return pltpu.make_async_remote_copy(
+            src_ref=db_ref.at[:, pl.ds(p * quarter, quarter), :],
+            dst_ref=share,
+            send_sem=base_send.at[p],
+            recv_sem=base_recv,
+            device_id={"pool": p},
+            device_id_type=MESH,
+        )
+
+    base_own = pltpu.make_async_copy(
+        db_ref.at[:, pl.ds(top * quarter, quarter), :], share, local_sem.at[0]
+    )
+
+    @pl.when(is_enc)
+    def _():
+        for p in range(top):
+            base_copy(p).start()
+        base_own.start()
+
+    lane = lax.broadcasted_iota(jnp.int32, (1, 128), 1)
+    line = jnp.zeros((1, 128), jnp.int32)
+    for k in range(per):
+        line = jnp.where(lane == k, owner_ref[k // nbr, k % nbr], line)
+        line = jnp.where(lane == per + k, block_ref[k // nbr, k % nbr], line)
+    for k in range(blocks):
+        line = jnp.where(lane == 2 * per + k, len_ref[0, k], line)
+    row[...] = line
+    metas[me, pool] = line
+
+    def row_copy(d):
+        return pltpu.make_async_remote_copy(
+            src_ref=row,
+            dst_ref=metas.at[me, pool],
+            send_sem=row_send.at[d],
+            recv_sem=row_recv.at[pools - d],
+            device_id={"pool": lax.rem(pool + d, pools)},
+            device_id_type=MESH,
+        )
+
+    for d in range(1, pools):
+        row_copy(d).start()
+    for d in range(1, pools):
+        row_copy(d).wait()
+
+    def meta_copy(d):
+        return pltpu.make_async_remote_copy(
+            src_ref=metas.at[me],
+            dst_ref=metas.at[me],
+            send_sem=meta_send.at[d],
+            recv_sem=meta_recv.at[columns - d],
+            device_id={"dp": lax.rem(me + d, columns)},
+            device_id_type=MESH,
+        )
+
+    def each(action):
+        def step(d, carry):
+            action(d)
+            return carry
+
+        lax.fori_loop(1, columns, step, 0)
+
+    each(lambda d: meta_copy(d).start())
+    each(lambda d: meta_copy(d).wait())
+    to_scalar = pltpu.make_async_copy(metas, smeta, local_sem.at[1])
+    to_scalar.start()
+    to_scalar.wait()
+
+    def find(j, carry):
+        first, last = jnp.int32(0), jnp.int32(0)
+        for q in range(top * per):
+            p, k = q // per, q % per
+            last = jnp.where(smeta[j, p, 0, k] == me, smeta[j, p, 0, per + k], last)
+            p, k = (top * per - 1 - q) // per, (top * per - 1 - q) % per
+            first = jnp.where(smeta[j, p, 0, k] == me, smeta[j, p, 0, per + k], first)
+        table[2 * j] = first
+        table[2 * j + 1] = last
+        return carry
+
+    lax.fori_loop(0, columns, find, 0)
+
+    @pl.when(is_enc)
+    def _():
+        base_own.wait()
+        for p in range(top):
+            base_copy(p).wait_send()
+
+    @pl.when(jnp.logical_not(is_enc))
+    def _():
+        base_copy(0).wait_recv()
+
+    def fill(j, carry):
+        for r in range(2):
+            send[j, r] = share[table[2 * j + r]]
+        return carry
+
+    lax.fori_loop(0, columns, fill, 0)
+    for r in range(2):
+        got[2 * me + r] = share[table[2 * me + r]]
+
+    def slot_copy(d):
+        to = lax.rem(me + d, columns)
+        return pltpu.make_async_remote_copy(
+            src_ref=send.at[to],
+            dst_ref=got.at[pl.ds(2 * me, 2)],
+            send_sem=slot_send.at[d],
+            recv_sem=slot_recv.at[columns - d],
+            device_id={"dp": to},
+            device_id_type=MESH,
+        )
+
+    each(lambda d: slot_copy(d).start())
+
+    named = [smeta[me, q // per, 0, q % per] for q in range(top * per)]
+    for q in range(top * per):
+        again = jnp.int32(0)
+        for e in range(q):
+            again = jnp.where(named[e] == named[q], 1, again)
+        place[q] = 2 * named[q] + again
+    mine = jnp.minimum(pool, top - 1)
+    for k in range(per):
+        info_ref[k] = smeta[smeta[me, mine, 0, k], top, 0, 2 * per + smeta[me, mine, 0, per + k]]
+    for k in range(per, info_ref.shape[0]):
+        info_ref[k] = is_enc.astype(jnp.int32)
+
+    each(lambda d: slot_copy(d).wait())
+
+    def choose(q, carry):
+        pick[q] = got[place[q]]
+        return carry
+
+    lax.fori_loop(0, top * per, choose, 0)
+
+    def pick_copy(p):
+        return pltpu.make_async_remote_copy(
+            src_ref=pick.at[pl.ds(p * per, per)],
+            dst_ref=out_ref.at[pool],
+            send_sem=pick_send.at[p],
+            recv_sem=pick_recv.at[pool],
+            device_id={"pool": p},
+            device_id_type=MESH,
+        )
+
+    def pick_from(p):
+        return pltpu.make_async_remote_copy(
+            src_ref=pick.at[pl.ds(0, per)],
+            dst_ref=out_ref.at[p],
+            send_sem=pick_send.at[p],
+            recv_sem=pick_recv.at[p],
+            device_id={"pool": p},
+            device_id_type=MESH,
+        )
+
+    pick_own = pltpu.make_async_copy(
+        pick.at[pl.ds(mine * per, per)], out_ref.at[pool], local_sem.at[2]
+    )
+    for p in range(top):
+
+        @pl.when(pool != p)
+        def _():
+            pick_copy(p).start()
+
+    pick_own.start()
+    pick_own.wait()
+    for p in range(top):
+
+        @pl.when(pool != p)
+        def _():
+            pick_copy(p).wait_send()
+
+    for p in range(pools):
+
+        @pl.when(jnp.logical_and(pool != p, jnp.logical_not(is_enc)))
+        def _():
+            pick_from(p).wait_recv()
+
+
+def fetch(pools, columns, nbr_owner, nbr_block, lengths, database):
+    blocks, slot_len, width = database.shape
+    per = nbr_owner.size
+    quarter = slot_len // pools
+    live = (pools - 1) * per
+    dma = pltpu.SemaphoreType.DMA
+    return pl.pallas_call(
+        functools.partial(fetch_kernel, pools, columns),
+        out_shape=(
+            jax.ShapeDtypeStruct((pools, per, quarter, width), BF16),
+            jax.ShapeDtypeStruct((2 * per,), jnp.int32),
+        ),
+        in_specs=[pl.BlockSpec(memory_space=pltpu.SMEM)] * 3
+        + [pl.BlockSpec(memory_space=pl.ANY)],
+        out_specs=(
+            pl.BlockSpec(memory_space=pltpu.VMEM),
+            pl.BlockSpec(memory_space=pltpu.SMEM),
+        ),
+        scratch_shapes=[
+            pltpu.VMEM((1, 128), jnp.int32),
+            pltpu.VMEM((columns, pools, 1, 128), jnp.int32),
+            pltpu.SMEM((columns, pools, 1, 128), jnp.int32),
+            pltpu.SMEM((2 * columns,), jnp.int32),
+            pltpu.SMEM((live,), jnp.int32),
+            pltpu.VMEM((blocks, quarter, width), BF16),
+            pltpu.VMEM((columns, 2, quarter, width), BF16),
+            pltpu.VMEM((2 * columns, quarter, width), BF16),
+            pltpu.VMEM((live, quarter, width), BF16),
+            dma((3,)),
+            dma((pools,)),
+            dma,
+            dma((pools,)),
+            dma((pools,)),
+            dma((columns,)),
+            dma((columns,)),
+            dma((columns,)),
+            dma((columns,)),
+            dma((pools,)),
+            dma((pools,)),
+        ],
+        compiler_params=pltpu.CompilerParams(
+            collective_id=0, has_side_effects=True, vmem_limit_bytes=40 << 20
+        ),
+        name="fetch",
+    )(nbr_owner, nbr_block, lengths, database)
+
+
+def sum_kernel(
+    pools, columns, part_ref, out_ref, lands, held, tops,
+    a_send, a_recv, b_send, b_recv,
+):
+    pool, me = lax.axis_index("pool"), lax.axis_index("dp")
+    top = pools - 1
+    is_dec = pool != top
+    greet(pools, columns)
+
+    def each(action):
+        def step(d, carry):
+            action(d)
+            return carry
+
+        lax.fori_loop(1, columns, step, 0)
+
+    def a_copy(d):
+        to = lax.rem(me + d, columns)
+        return pltpu.make_async_remote_copy(
+            src_ref=part_ref.at[to],
+            dst_ref=lands.at[me],
+            send_sem=a_send.at[d],
+            recv_sem=a_recv.at[columns - d],
+            device_id={"dp": to},
+            device_id_type=MESH,
+        )
+
+    def b_copy(p):
+        return pltpu.make_async_remote_copy(
+            src_ref=held.at[p],
+            dst_ref=tops.at[pool],
+            send_sem=b_send.at[p],
+            recv_sem=b_recv.at[pool],
+            device_id={"pool": p},
+            device_id_type=MESH,
+        )
+
+    def b_from(p):
+        return pltpu.make_async_remote_copy(
+            src_ref=held.at[p],
+            dst_ref=tops.at[p],
+            send_sem=b_send.at[p],
+            recv_sem=b_recv.at[p],
+            device_id={"pool": p},
+            device_id_type=MESH,
+        )
+
+    @pl.when(is_dec)
+    def _():
+        each(lambda d: a_copy(d).start())
+        lands[me] = part_ref[me]
+        each(lambda d: a_copy(d).wait())
+
+        def add(j, total):
+            return total + lands[j]
+
+        held[...] = lax.fori_loop(1, columns, add, lands[0])
+        for p in range(pools):
+
+            @pl.when(pool != p)
+            def _():
+                b_copy(p).start()
+
+            @pl.when(pool == p)
+            def _():
+                tops[p] = held[p]
+
+        for p in range(pools):
+
+            @pl.when(pool != p)
+            def _():
+                b_copy(p).wait_send()
+
+    for p in range(top):
+
+        @pl.when(pool != p)
+        def _():
+            b_from(p).wait_recv()
+
+    total = tops[0]
+    for p in range(1, top):
+        total = total + tops[p]
+    out_ref[...] = total
+
+
+def sum_parts(pools, columns, parts):
+    rows, width = parts.shape[2:]
+    dma = pltpu.SemaphoreType.DMA
+    return pl.pallas_call(
+        functools.partial(sum_kernel, pools, columns),
+        out_shape=jax.ShapeDtypeStruct((rows, width), F32),
+        in_specs=[pl.BlockSpec(memory_space=pltpu.VMEM)],
+        out_specs=pl.BlockSpec(memory_space=pltpu.VMEM),
+        scratch_shapes=[
+            pltpu.VMEM(parts.shape, F32),
+            pltpu.VMEM((pools, rows, width), F32),
+            pltpu.VMEM((pools, rows, width), F32),
+            dma((columns,)),
+            dma((columns,)),
+            dma((pools,)),
+            dma((pools,)),
+        ],
+        compiler_params=pltpu.CompilerParams(
+            collective_id=1, has_side_effects=True, vmem_limit_bytes=24 << 20
+        ),
+        name="sum_parts",
+    )(parts)
 
 
 def body(
@@ -157,84 +538,34 @@
 ):
     pools = lax.axis_size("pool")
     columns = lax.axis_size("dp")
-    relay_row = pools - 1
-    pool_index = lax.axis_index("pool")
-    me = lax.axis_index("dp")
-    on_encoder = pool_index == relay_row
-    span_count = cond.shape[2]
-    enc_width = cond.shape[3]
-    nbr_count = nbr_owner.shape[3]
-    per_device = span_count * nbr_count
-    blk_dev = database.shape[2]
-    slot_len = database.shape[3]
-    token_count = queries.shape[2]
-    head_cols = queries.shape[3]
-    quarter = slot_len // pools
-
-    meta = jnp.concatenate([nbr_owner.reshape(-1), nbr_block.reshape(-1), lengths.reshape(-1)])
-    meta = jnp.broadcast_to(meta[None], (pools * columns,) + meta.shape)
-    meta = lax.all_to_all(meta, ("pool", "dp"), split_axis=0, concat_axis=0, tiled=True)
-    meta = meta.reshape(pools, columns, -1)
-    owner = jnp.swapaxes(meta[:relay_row, :, :per_device], 0, 1).reshape(columns, -1)
-    block = jnp.swapaxes(meta[:relay_row, :, per_device : 2 * per_device], 0, 1).reshape(
-        columns, -1
+    tokens, hq = queries.shape[2:]
+    spans, width = cond.shape[2:]
+    blocks, info = fetch(
+        pools,
+        columns,
+        nbr_owner.reshape(nbr_owner.shape[2:]),
+        nbr_block.reshape(nbr_block.shape[2:]),
+        lengths.reshape(1, -1),
+        database.reshape(database.shape[2:]),
     )
-    lens = meta[relay_row, :, 2 * per_device :]
-
-    db4 = database.reshape(blk_dev, pools, quarter, enc_width)
-    db4 = jnp.swapaxes(db4, 0, 1)
-    mine = lax.all_to_all(db4, "pool", split_axis=0, concat_axis=0, tiled=True)[relay_row]
-
-    live = owner.shape[1]
-    order = jnp.arange(live, dtype=jnp.int32)[None, :]
-    named = owner == me
-    first = jnp.min(jnp.where(named, order, live), axis=1, keepdims=True)
-    last = jnp.max(jnp.where(named, order, -1), axis=1, keepdims=True)
-    b0 = jnp.sum(jnp.where(order == first, block, 0), axis=1)
-    b1 = jnp.sum(jnp.where(order == last, block, 0), axis=1)
-    slot_block = jnp.stack([b0, b1], axis=1).reshape(-1)
-    send = jnp.take(mine, slot_block, axis=0).reshape(columns, 2, quarter, enc_width)
-
-    got = lax.all_to_all(send, "dp", split_axis=0, concat_axis=0, tiled=True)
-    got = got.reshape(columns * 2, quarter, enc_width)
-
-    my_owner = lax.dynamic_index_in_dim(owner, me, 0, keepdims=False)
-    my_block = lax.dynamic_index_in_dim(block, me, 0, keepdims=False)
-    earlier = jnp.tril(jnp.ones((live, live), jnp.int32), -1)
-    later = jnp.max(
-        jnp.where(my_owner[:, None] == my_owner[None, :], earlier, 0), axis=1
-    )
-    position = my_owner * 2 + later
-    pick = jnp.take(got, position, axis=0).reshape(relay_row, per_device, quarter, enc_width)
-    pick = jnp.concatenate([pick, pick[:1]], axis=0)
-    blocks = lax.all_to_all(pick, "pool", split_axis=0, concat_axis=0, tiled=True)
-
-    own_row = jnp.minimum(pool_index, relay_row - 1)
-    dec_owner = lax.dynamic_slice_in_dim(my_owner, own_row * per_device, per_device, 0)
-    dec_block = lax.dynamic_slice_in_dim(my_block, own_row * per_device, per_device, 0)
-    my_len = jnp.take(lens.reshape(-1), dec_owner * blk_dev + dec_block)
-
-    info = jnp.concatenate([my_len, on_encoder.astype(jnp.int32)[None]])
-    attn_out, q_grad, cond_grad, adapter = attend(
+    attn_out, q_grad, cond_grad, parts = attend(
+        columns,
         info,
-        queries.reshape(token_count, head_cols),
-        cotangent.reshape(token_count, head_cols),
+        queries.reshape(tokens, hq),
+        cotangent.reshape(tokens, hq),
         blocks,
-        cond.reshape(span_count, enc_width),
+        cond.reshape(spans, width),
         gain,
         w_down,
         w_up,
         w_kv,
         unroll=4,
     )
-    parts = pools * columns
-    adapter = adapter.reshape(parts, enc_width // parts, -1)
-    adapter = lax.all_to_all(adapter, ("pool", "dp"), split_axis=0, concat_axis=0, tiled=True)
-    adapter_grad = jnp.sum(adapter, axis=0)
+    adapter_grad = sum_parts(pools, columns, parts)
     return (
-        attn_out.reshape(1, 1, token_count, head_cols),
-        q_grad.reshape(1, 1, token_count, head_cols),
-        cond_grad.reshape(1, 1, span_count, enc_width),
+        attn_out.reshape(1, 1, tokens, hq),
+        q_grad.reshape(1, 1, tokens, hq),
+        cond_grad.reshape(1, 1, spans, width),
         adapter_grad,
     )
 

time: 192 us -> 153 us (0.80)
  Pallas kernels: 50.9 us -> 144 us
  waiting for transfers between devices: 71.8 us -> 0 us
  starting transfers between devices: 26.8 us -> 0 us
  blocking collectives: 24.4 us -> 0 us
  other arithmetic: 5.89 us -> 0 us
  local copies, waits for them, and re-layouts: 10.9 us -> 7.07 us
    pallas_call x0 -> x2, Pallas kernels: none -> 92.6 us  [the longest x1 67.7 us: fetch(): pl.pallas_call(functools.partial(fetch_kernel, pools, columns), out_shape...]
    all_to_all x4 -> x0, waiting for transfers between devices: 71.8 us -> none  [the longest x1 26.5 us: body(): got = lax.all_to_all(send, 'dp', split_axis=0, concat_axis=0, tiled=True)]
    all_to_all x4 -> x0, starting transfers between devices: 26.8 us -> none  [the longest x1 11.5 us: body(): lax.all_to_all(meta, ('pool', 'dp'), split_axis=0, concat_axis=0, tiled=T...]
    all_to_all x1 -> x0, blocking collectives: 24.4 us -> none  [body(): lax.all_to_all(adapter, ('pool', 'dp'), split_axis=0, concat_axis=0, tile...]
    transpose x1 -> x0, local copies, waits for them, and re-layouts: 3.19 us -> none  [body(): db4 = jnp.swapaxes(db4, 0, 1)]
    unnamed x6 -> x11, local copies, waits for them, and re-layouts: 2.68 us -> 5.54 us
    concatenate x3 -> x0, other arithmetic: 2.39 us -> none  [the longest x1 1.06 us: body(): pick = jnp.concatenate([pick, pick[:1]], axis=0)]
    gather x3 -> x0, local copies, waits for them, and re-layouts: 1.92 us -> none  [the longest x1 0.68 us: body(): jnp.take(mine, slot_block, axis=0).reshape(columns, 2, quarter, enc_width)]
  transfers between devices with their start and end apart: 4 -> 0, of which waited for: 4 -> 0; matrix products, arithmetic and copies ran while one was open for 3% -> 0% of each run, Pallas kernels for 0% -> 0%
where the time goes in v3:
time: 153 us; the launch traced here: 151 us
  Pallas kernels  144 us (94%)
  local copies, waits for them, and re-layouts  7.07 us (5%)
    pallas_call x1, Pallas kernels, fetch(): pl.pallas_call(functools.partial(fetch_kernel, pools, columns), out_shape...  67.7 us
    pallas_call x1, Pallas kernels, attend(): pl.pallas_call(functools.partial(attend_kernel, unroll), out_shape=(jax.S...  51 us
    pallas_call x1, Pallas kernels, sum_parts(): pl.pallas_call(functools.partial(sum_kernel, pools, columns), out_shape=j...  24.9 us
    unnamed x11, local copies, waits for them, and re-layouts  5.54 us

profile of v3, /device:TPU:1, one launch (start us, length us, event | category | flops | bytes accessed | tf_op | source)
XLA Modules:
  0.0 151.3 jit_solution(14362226127708681336)
XLA Ops:
  0.6 0.8 copy.15.owner_ref
  1.4 0.8 copy.16.block_ref
  2.2 0.0 copy-start
  2.2 1.6 %copy-done = bf16[1,1,16,128,512]{4,3,2,1,0:T(8,128)(2,1)S(1)} copy-done((bf16[1,1,16,128,512]{4,3,2,1,0:T(8,128)(2,1)S(1)}, bf16[1,1,16,128,512]{4,3,2,1,0:T(8,128)(2,1)}, u32[]{:S(2)}) %copy-start) | copy-done | bytes 2097176
  3.8 0.0 copy-start.3
  3.8 0.7 copy-done.3
  4.4 67.7 %fetch.1 = (bf16[4,8,32,512]{3,2,1,0:T(8,128)(2,1)S(1)}, s32[16]{0:T(128)S(1)}) custom-call(s32[4,2]{1,0:T(4,128)S(1)} %copy.15.owner_ref, s32[4,2]{1,0:T(4,128)S(1)} %copy.16.block_ref, s32[1,16]{1,0:T(1,128)S(1)} %bitcast.12, bf16[16,128,512]{2,1,0:T(8,128)(2,1)S(1)} %bitcast.11), custom_call_target="tpu_custom_call" | custom-call | tf_op jit(solution)/shard_map/fetch/pallas_call | solution.py:386
  72.1 0.0 copy-start.1
  72.1 1.0 copy-done.1
  73.1 0.0 copy-start.4
  73.1 0.5 copy-done.4
  73.6 51.0 %attend.1 = (bf16[256,2048]{1,0:T(8,128)(2,1)}, bf16[256,2048]{1,0:T(8,128)(2,1)}, f32[4,512]{1,0:T(4,128)}, f32[32,4,4,512]{3,2,1,0:T(4,128)}) custom-call(s32[16]{0:T(128)} %copy-done.4, bf16[256,2048]{1,0:T(8,128)(2,1)} %bitcast.13, bf16[256,2048]{1,0:T(8,128)(2,1)} %bitcast.14, bf16[4,8,32,512]{3,2,1,0:T(8,128)(2,1)} %copy-done.1, ...), custom_call_target="tpu_custom_call" | custom-call | tf_op jit(solution)/shard_map/attend/pallas_call | solution.py:128
  124.6 0.0 copy-start.2
  124.6 1.2 copy-done.2
  125.8 24.9 %sum_parts.1 = f32[4,512]{1,0:T(4,128)S(1)} custom-call(f32[32,4,4,512]{3,2,1,0:T(4,128)S(1)} %copy-done.2), custom_call_target="tpu_custom_call" | custom-call | tf_op jit(solution)/shard_map/sum_parts/pallas_call | solution.py:515
  150.7 0.6 copy.18
Async XLA Ops:
  2.2 1.6 %copy-start = (bf16[1,1,16,128,512]{4,3,2,1,0:T(8,128)(2,1)S(1)}, bf16[1,1,16,128,512]{4,3,2,1,0:T(8,128)(2,1)}, u32[]{:S(2)}) copy-start(bf16[1,1,16,128,512]{4,3,2,1,0:T(8,128)(2,1)} %param.16) | copy-start | bytes 6291460
  3.8 0.7 copy-start.3
  72.1 1.0 copy-start.1
  73.1 0.5 copy-start.4
  124.6 1.2 copy-start.2

commit v4 on v3

--- a/solution.py
+++ b/solution.py
@@ -73,32 +73,38 @@
         bound = jnp.where(slot < slot_len, info[c * nbr], info[c * nbr + 1] + slot_len)
         usable = slot < bound
 
-        def head(h):
-            qs = pl.ds(pl.multiple_of(h * HEAD, HEAD), HEAD)
-            vs = pl.ds(pl.multiple_of(hq + h * HEAD, HEAD), HEAD)
-            q = q_ref[:, qs]
-            do = do_ref[:, qs]
-            k = kv[:, qs]
-            v = kv[:, vs]
-            s = jnp.where(usable, dot_nt(q, k) * scaling, FLOOR)
-            dp = dot_nt(do, v)
+        def score(h):
+            qs = pl.ds(h * HEAD, HEAD)
+            vs = pl.ds(hq + h * HEAD, HEAD)
+            s = dot_nt(q_ref[:, qs], kv[:, qs])
+            dp = dot_nt(do_ref[:, qs], kv[:, vs])
+            return s, dp
+
+        def weigh(s, dp):
+            s = jnp.where(usable, s * scaling, FLOOR)
             e = jnp.exp(s - jnp.max(s, axis=-1, keepdims=True))
             p = e * (1.0 / jnp.sum(e, axis=-1, keepdims=True))
-            pb = p.astype(BF16)
             pdp = p * dp
             delta = jnp.sum(pdp, axis=-1, keepdims=True)
-            ds = (pdp - p * delta).astype(BF16)
-            out_ref[:, qs] = dot_nn(pb, v).astype(BF16)
-            dq_ref[:, qs] = (dot_nn(ds, k) * scaling).astype(BF16)
-            kvg[:, qs] = (dot_tn(ds, q) * scaling).astype(BF16)
-            kvg[:, vs] = dot_tn(pb, do).astype(BF16)
-
-        def heads(i, carry):
-            for u in range(unroll):
-                head(i * unroll + u)
-            return carry
-
-        lax.fori_loop(0, hq // HEAD // unroll, heads, 0)
+            return p.astype(BF16), (pdp - p * delta).astype(BF16)
+
+        def finish(h, pb, ds):
+            qs = pl.ds(h * HEAD, HEAD)
+            vs = pl.ds(hq + h * HEAD, HEAD)
+            out_ref[:, qs] = dot_nn(pb, kv[:, vs]).astype(BF16)
+            dq_ref[:, qs] = (dot_nn(ds, kv[:, qs]) * scaling).astype(BF16)
+            kvg[:, qs] = (dot_tn(ds, q_ref[:, qs]) * scaling).astype(BF16)
+            kvg[:, vs] = dot_tn(pb, do_ref[:, qs]).astype(BF16)
+
+        heads = hq // HEAD
+        first, second = {}, {}
+        for i in range(heads + 2 * unroll):
+            if i < heads:
+                first[i] = score(i)
+            if 0 <= i - unroll < heads:
+                second[i - unroll] = weigh(*first.pop(i - unroll))
+            if 0 <= i - 2 * unroll < heads:
+                finish(i - 2 * unroll, *second.pop(i - 2 * unroll))
 
         enc_grad = dot_nt(kvg[...], wkv_ref[...]).astype(BF16)
         lat_grad = dot_nt(enc_grad, wu_ref[...]).astype(BF16)
@@ -114,7 +120,7 @@
         columns, pools_out, piece, _ = part_ref.shape
         for p in range(pools_out):
             for j in range(columns):
-                part_ref[j, p] = ad_ref[pl.ds((p * columns + j) * piece, piece), :]
+                part_ref[j, p] = ad_ref[pl.ds((p * columns + j) * piece, piece), :].astype(BF16)
 
 
 def attend(columns, info, queries, cotangent, blocks, cond, gain, w_down, w_up, w_kv, unroll=2):
@@ -131,7 +137,7 @@
             jax.ShapeDtypeStruct((tokens, hq), BF16),
             jax.ShapeDtypeStruct((tokens, hq), BF16),
             jax.ShapeDtypeStruct((spans, width), F32),
-            jax.ShapeDtypeStruct((columns, pools, width // (pools * columns), 2 * rank), F32),
+            jax.ShapeDtypeStruct((columns, pools, width // (pools * columns), 2 * rank), BF16),
         ),
         grid_spec=pltpu.PrefetchScalarGridSpec(
             num_scalar_prefetch=1,
@@ -188,7 +194,7 @@
 
 def fetch_kernel(
     pools, columns, owner_ref, block_ref, len_ref, db_ref, out_ref, info_ref,
-    row, metas, smeta, table, place, share, send, got, pick,
+    row, metas, smeta, found, table, place, share, send, got, pick,
     local_sem, base_send, base_recv, row_send, row_recv, meta_send, meta_recv,
     slot_send, slot_recv, pick_send, pick_recv,
 ):
@@ -214,12 +220,6 @@
         db_ref.at[:, pl.ds(top * quarter, quarter), :], share, local_sem.at[0]
     )
 
-    @pl.when(is_enc)
-    def _():
-        for p in range(top):
-            base_copy(p).start()
-        base_own.start()
-
     lane = lax.broadcasted_iota(jnp.int32, (1, 128), 1)
     line = jnp.zeros((1, 128), jnp.int32)
     for k in range(per):
@@ -263,23 +263,32 @@
         lax.fori_loop(1, columns, step, 0)
 
     each(lambda d: meta_copy(d).start())
+
+    @pl.when(is_enc)
+    def _():
+        for p in range(top):
+            base_copy(p).start()
+        base_own.start()
+
     each(lambda d: meta_copy(d).wait())
     to_scalar = pltpu.make_async_copy(metas, smeta, local_sem.at[1])
     to_scalar.start()
-    to_scalar.wait()
-
-    def find(j, carry):
-        first, last = jnp.int32(0), jnp.int32(0)
-        for q in range(top * per):
-            p, k = q // per, q % per
-            last = jnp.where(smeta[j, p, 0, k] == me, smeta[j, p, 0, per + k], last)
-            p, k = (top * per - 1 - q) // per, (top * per - 1 - q) % per
-            first = jnp.where(smeta[j, p, 0, k] == me, smeta[j, p, 0, per + k], first)
-        table[2 * j] = first
-        table[2 * j + 1] = last
-        return carry
-
-    lax.fori_loop(0, columns, find, 0)
+
+    lanes = lax.broadcasted_iota(jnp.int32, (columns, 128), 1)
+    least = jnp.full((columns, 128), blocks << 16, jnp.int32)
+    most = jnp.zeros((columns, 128), jnp.int32)
+    for p in range(top):
+        lists = metas[:, p, 0, :]
+        key = (lanes + (p * per + 1)) * blocks + pltpu.roll(lists, 128 - per, 1)
+        named = jnp.logical_and(lists == me, lanes < per)
+        least = jnp.minimum(least, jnp.where(named, key, blocks << 16))
+        most = jnp.maximum(most, jnp.where(named, key, 0))
+    least = jnp.bitwise_and(jnp.min(least, axis=1, keepdims=True), blocks - 1)
+    most = jnp.bitwise_and(jnp.max(most, axis=1, keepdims=True), blocks - 1)
+    found[...] = jnp.where(lanes == 0, least, most)
+    to_table = pltpu.make_async_copy(found, table, local_sem.at[2])
+    to_table.start()
+    to_table.wait()
 
     @pl.when(is_enc)
     def _():
@@ -293,12 +302,12 @@
 
     def fill(j, carry):
         for r in range(2):
-            send[j, r] = share[table[2 * j + r]]
+            send[j, r] = share[table[j, r]]
         return carry
 
     lax.fori_loop(0, columns, fill, 0)
     for r in range(2):
-        got[2 * me + r] = share[table[2 * me + r]]
+        got[2 * me + r] = share[table[me, r]]
 
     def slot_copy(d):
         to = lax.rem(me + d, columns)
@@ -313,6 +322,7 @@
 
     each(lambda d: slot_copy(d).start())
 
+    to_scalar.wait()
     named = [smeta[me, q // per, 0, q % per] for q in range(top * per)]
     for q in range(top * per):
         again = jnp.int32(0)
@@ -354,7 +364,7 @@
         )
 
     pick_own = pltpu.make_async_copy(
-        pick.at[pl.ds(mine * per, per)], out_ref.at[pool], local_sem.at[2]
+        pick.at[pl.ds(mine * per, per)], out_ref.at[pool], local_sem.at[3]
     )
     for p in range(top):
 
@@ -399,13 +409,14 @@
             pltpu.VMEM((1, 128), jnp.int32),
             pltpu.VMEM((columns, pools, 1, 128), jnp.int32),
             pltpu.SMEM((columns, pools, 1, 128), jnp.int32),
-            pltpu.SMEM((2 * columns,), jnp.int32),
+            pltpu.VMEM((columns, 128), jnp.int32),
+            pltpu.SMEM((columns, 128), jnp.int32),
             pltpu.SMEM((live,), jnp.int32),
             pltpu.VMEM((blocks, quarter, width), BF16),
             pltpu.VMEM((columns, 2, quarter, width), BF16),
             pltpu.VMEM((2 * columns, quarter, width), BF16),
             pltpu.VMEM((live, quarter, width), BF16),
-            dma((3,)),
+            dma((4,)),
             dma((pools,)),
             dma,
             dma((pools,)),
@@ -478,9 +489,9 @@
         each(lambda d: a_copy(d).wait())
 
         def add(j, total):
-            return total + lands[j]
-
-        held[...] = lax.fori_loop(1, columns, add, lands[0])
+            return total + lands[j].astype(F32)
+
+        held[...] = lax.fori_loop(1, columns, add, lands[0].astype(F32))
         for p in range(pools):
 
             @pl.when(pool != p)
@@ -518,7 +529,7 @@
         in_specs=[pl.BlockSpec(memory_space=pltpu.VMEM)],
         out_specs=pl.BlockSpec(memory_space=pltpu.VMEM),
         scratch_shapes=[
-            pltpu.VMEM(parts.shape, F32),
+            pltpu.VMEM(parts.shape, BF16),
             pltpu.VMEM((pools, rows, width), F32),
             pltpu.VMEM((pools, rows, width), F32),
             dma((columns,)),

time: 153 us -> 112 us (0.73)
  Pallas kernels: 144 us -> 103 us
    pallas_call x1, Pallas kernels: 51 us -> 26 us  [attend(): pl.pallas_call(functools.partial(attend_kernel, unroll), out_shape=(jax.S...]
    pallas_call x1, Pallas kernels: 24.9 us -> 14.1 us  [sum_parts(): pl.pallas_call(functools.partial(sum_kernel, pools, columns), out_shape=j...]
    pallas_call x1, Pallas kernels: 67.7 us -> 63.1 us  [fetch(): pl.pallas_call(functools.partial(fetch_kernel, pools, columns), out_shape...]
where the time goes in v4:
time: 112 us; the launch traced here: 111 us
  Pallas kernels  103 us (92%)
  local copies, waits for them, and re-layouts  6.88 us (6%)
    pallas_call x1, Pallas kernels, fetch(): pl.pallas_call(functools.partial(fetch_kernel, pools, columns), out_shape...  63.1 us
    pallas_call x1, Pallas kernels, attend(): pl.pallas_call(functools.partial(attend_kernel, unroll), out_shape=(jax.S...  26 us
    pallas_call x1, Pallas kernels, sum_parts(): pl.pallas_call(functools.partial(sum_kernel, pools, columns), out_shape=j...  14.1 us
    unnamed x11, local copies, waits for them, and re-layouts  5.35 us

profile of v4, /device:TPU:1, one launch (start us, length us, event | category | flops | bytes accessed | tf_op | source)
XLA Modules:
  0.0 110.7 jit_solution(14773836356894259112)
XLA Ops:
  0.6 0.8 copy.15.owner_ref
  1.4 0.8 copy.16.block_ref
  2.2 0.0 copy-start
  2.2 1.6 %copy-done = bf16[1,1,16,128,512]{4,3,2,1,0:T(8,128)(2,1)S(1)} copy-done((bf16[1,1,16,128,512]{4,3,2,1,0:T(8,128)(2,1)S(1)}, bf16[1,1,16,128,512]{4,3,2,1,0:T(8,128)(2,1)}, u32[]{:S(2)}) %copy-start) | copy-done | bytes 2097176
  3.8 0.0 copy-start.3
  3.8 0.7 copy-done.3
  4.4 63.1 %fetch.1 = (bf16[4,8,32,512]{3,2,1,0:T(8,128)(2,1)S(1)}, s32[16]{0:T(128)S(1)}) custom-call(s32[4,2]{1,0:T(4,128)S(1)} %copy.15.owner_ref, s32[4,2]{1,0:T(4,128)S(1)} %copy.16.block_ref, s32[1,16]{1,0:T(1,128)S(1)} %bitcast.12, bf16[16,128,512]{2,1,0:T(8,128)(2,1)S(1)} %bitcast.11), custom_call_target="tpu_custom_call" | custom-call | tf_op jit(solution)/shard_map/fetch/pallas_call | solution.py:396
  67.5 0.0 copy-start.1
  67.5 1.0 copy-done.1
  68.5 0.0 copy-start.4
  68.5 0.5 copy-done.4
  69.0 26.0 %attend.1 = (bf16[256,2048]{1,0:T(8,128)(2,1)}, bf16[256,2048]{1,0:T(8,128)(2,1)}, f32[4,512]{1,0:T(4,128)}, bf16[32,4,4,512]{3,2,1,0:T(4,128)(2,1)}) custom-call(s32[16]{0:T(128)} %copy-done.4, bf16[256,2048]{1,0:T(8,128)(2,1)} %bitcast.13, bf16[256,2048]{1,0:T(8,128)(2,1)} %bitcast.14, bf16[4,8,32,512]{3,2,1,0:T(8,128)(2,1)} %copy-done.1, ...), custom_call_target="tpu_custom_call" | custom-call | tf_op jit(solution)/shard_map/attend/pallas_call | solution.py:134
  95.0 0.0 copy-start.2
  95.0 1.0 copy-done.2
  96.0 14.1 %sum_parts.1 = f32[4,512]{1,0:T(4,128)S(1)} custom-call(bf16[32,4,4,512]{3,2,1,0:T(4,128)(2,1)S(1)} %copy-done.2), custom_call_target="tpu_custom_call" | custom-call | tf_op jit(solution)/shard_map/sum_parts/pallas_call | solution.py:526
  110.1 0.6 copy.18
Async XLA Ops:
  2.2 1.6 %copy-start = (bf16[1,1,16,128,512]{4,3,2,1,0:T(8,128)(2,1)S(1)}, bf16[1,1,16,128,512]{4,3,2,1,0:T(8,128)(2,1)}, u32[]{:S(2)}) copy-start(bf16[1,1,16,128,512]{4,3,2,1,0:T(8,128)(2,1)} %param.16) | copy-start | bytes 6291460
  3.8 0.7 copy-start.3
  67.5 1.0 copy-start.1
  68.5 0.5 copy-start.4
  95.0 1.0 copy-start.2

commit v5 on v2

v5 whole, which is shorter than its diff:
```python
import functools

import jax
import jax.numpy as jnp
from jax import lax
from jax.experimental import pallas as pl
from jax.experimental.pallas import tpu as pltpu
from jax.sharding import PartitionSpec as P

HEAD = 128
SPAN = 64
EPSILON = 1e-06
FLOOR = -1e30
STAGE = 4
F32 = jnp.float32
BF16 = jnp.bfloat16
MESH = pl.DeviceIdType.MESH


def dot_nn(a, b):
    return lax.dot_general(a, b, (((1,), (0,)), ((), ())), preferred_element_type=F32)


def dot_nt(a, b):
    return lax.dot_general(a, b, (((1,), (1,)), ((), ())), preferred_element_type=F32)


def dot_tn(a, b):
    return lax.dot_general(a, b, (((0,), (0,)), ((), ())), preferred_element_type=F32)


def greet(pools, columns):
    pool, me = lax.axis_index("pool"), lax.axis_index("dp")
    barrier = pltpu.get_barrier_semaphore()

    def hello(d, carry):
        pl.semaphore_signal(
            barrier, inc=1, device_id={"dp": lax.rem(me + d, columns)}, device_id_type=MESH
        )
        return carry

    lax.fori_loop(1, columns, hello, 0)
    for d in range(1, pools):
        pl.semaphore_signal(
            barrier, inc=1, device_id={"pool": lax.rem(pool + d, pools)}, device_id_type=MESH
        )
    pl.semaphore_wait(barrier, columns - 1 + pools - 1)


def whole_kernel(
    pools, columns,
    owner_ref, block_ref, len_ref, db_ref, q_hbm, do_hbm, cond_ref, gain_ref, wd_hbm, wu_hbm,
    wkv_hbm,
    out_ref, dq_ref, cg_ref, sum_ref,
    row, metas, smeta, found, table, place, lens, share, send, got, pick, blk,
    q_ref, do_ref, wd_ref, wu_ref, wkv_ref, kv, kvg, ad_ref, part, lands, held, tops,
    load_sem, local_sem, base_send, base_recv, row_send, row_recv, meta_send, meta_recv,
    slot_send, slot_recv, pick_send, pick_recv, a_send, a_recv, b_send, b_recv,
):
    pool, me = lax.axis_index("pool"), lax.axis_index("dp")
    top = pools - 1
    nbr, spans = owner_ref.shape
    per = spans * nbr
    blocks, quarter, width = share.shape
    hq = q_ref.shape[1]
    rank = wd_ref.shape[1]
    slot_len = pools * quarter
    is_enc = pool == top
    is_dec = jnp.logical_not(is_enc)

    loads = [
        pltpu.make_async_copy(a, b, load_sem.at[i])
        for i, (a, b) in enumerate(
            ((wd_hbm, wd_ref), (wu_hbm, wu_ref), (wkv_hbm, wkv_ref), (q_hbm, q_ref), (do_hbm, do_ref))
        )
    ]

    @pl.when(is_dec)
    def _():
        for load in loads:
            load.start()

    def each(action):
        def step(d, carry):
            action(d)
            return carry

        lax.fori_loop(1, columns, step, 0)

    lane = lax.broadcasted_iota(jnp.int32, (1, 128), 1)
    line = jnp.zeros((1, 128), jnp.int32)
    for k in range(per):
        line = jnp.where(lane == k, owner_ref[k % nbr, k // nbr], line)
        line = jnp.where(lane == per + k, block_ref[k % nbr, k // nbr], line)
    for k in range(blocks):
        line = jnp.where(lane == 2 * per + k, len_ref[0, k], line)
    row[...] = line
    metas[me, pool] = line
    greet(pools, columns)

    def row_copy(d):
        return pltpu.make_async_remote_copy(
            src_ref=row,
            dst_ref=metas.at[me, pool],
            send_sem=row_send.at[d],
            recv_sem=row_recv.at[pools - d],
            device_id={"pool": lax.rem(pool + d, pools)},
            device_id_type=MESH,
        )

    for d in range(1, pools):
        row_copy(d).start()
    for d in range(1, pools):
        row_copy(d).wait()

    def meta_copy(d):
        return pltpu.make_async_remote_copy(
            src_ref=metas.at[me],
            dst_ref=metas.at[me],
            send_sem=meta_send.at[d],
            recv_sem=meta_recv.at[columns - d],
            device_id={"dp": lax.rem(me + d, columns)},
            device_id_type=MESH,
        )

    each(lambda d: meta_copy(d).start())

    def base_copy(p):
        return pltpu.make_async_remote_copy(
            src_ref=db_ref.at[:, pl.ds(p * quarter, quarter), :],
            dst_ref=share,
            send_sem=base_send.at[p],
            recv_sem=base_recv,
            device_id={"pool": p},
            device_id_type=MESH,
        )

    base_own = pltpu.make_async_copy(
        db_ref.at[:, pl.ds(top * quarter, quarter), :], share, local_sem.at[0]
    )

    @pl.when(is_enc)
    def _():
        for p in range(top):
            base_copy(p).start()
        base_own.start()

    each(lambda d: meta_copy(d).wait())
    to_scalar = pltpu.make_async_copy(metas, smeta, local_sem.at[1])
    to_scalar.start()

    lanes = lax.broadcasted_iota(jnp.int32, (columns, 128), 1)
    least = jnp.full((columns, 128), blocks << 16, jnp.int32)
    most = jnp.zeros((columns, 128), jnp.int32)
    for p in range(top):
        lists = metas[:, p, 0, :]
        key = (lanes + (p * per + 1)) * blocks + pltpu.roll(lists, 128 - per, 1)
        named = jnp.logical_and(lists == me, lanes < per)
        least = jnp.minimum(least, jnp.where(named, key, blocks << 16))
        most = jnp.maximum(most, jnp.where(named, key, 0))
    least = jnp.bitwise_and(jnp.min(least, axis=1, keepdims=True), blocks - 1)
    most = jnp.bitwise_and(jnp.max(most, axis=1, keepdims=True), blocks - 1)
    found[...] = jnp.where(lanes == 0, least, most)
    to_table = pltpu.make_async_copy(found, table, local_sem.at[2])
    to_table.start()
    to_table.wait()

    @pl.when(is_enc)
    def _():
        base_own.wait()

    @pl.when(is_dec)
    def _():
        base_copy(0).wait_recv()

    def fill(j, carry):
        for r in range(2):
            send[j, r] = share[table[j, r]]
        return carry

    lax.fori_loop(0, columns, fill, 0)
    for r in range(2):
        got[2 * me + r] = share[table[me, r]]

    def slot_copy(d):
        to = lax.rem(me + d, columns)
        return pltpu.make_async_remote_copy(
            src_ref=send.at[to],
            dst_ref=got.at[pl.ds(2 * me, 2)],
            send_sem=slot_send.at[d],
            recv_sem=slot_recv.at[columns - d],
            device_id={"dp": to},
            device_id_type=MESH,
        )

    each(lambda d: slot_copy(d).start())

    to_scalar.wait()
    names = [smeta[me, q // per, 0, q % per] for q in range(top * per)]
    for q in range(top * per):
        again = jnp.int32(0)
        for e in range(q):
            again = jnp.where(names[e] == names[q], 1, again)
        place[q] = 2 * names[q] + again
    mine = jnp.minimum(pool, top - 1)
    for k in range(per):
        lens[k] = smeta[smeta[me, mine, 0, k], top, 0, 2 * per + smeta[me, mine, 0, per + k]]

    ad_ref[...] = jnp.zeros_like(ad_ref)
    cg_ref[...] = jnp.zeros_like(cg_ref)

    @pl.when(is_enc)
    def _():
        out_ref[...] = jnp.zeros_like(out_ref)
        dq_ref[...] = jnp.zeros_like(dq_ref)
        for p in range(top):
            base_copy(p).wait_send()

    each(lambda d: slot_copy(d).wait_recv())

    def pick_copy(p, c):
        return pltpu.make_async_remote_copy(
            src_ref=pick.at[pl.ds(p * per + c * nbr, nbr)],
            dst_ref=blk.at[pool, pl.ds(c * nbr, nbr)],
            send_sem=pick_send.at[c, p],
            recv_sem=pick_recv.at[c, pool],
            device_id={"pool": p},
            device_id_type=MESH,
        )

    def pick_from(p, c):
        return pltpu.make_async_remote_copy(
            src_ref=pick.at[pl.ds(0, nbr)],
            dst_ref=blk.at[p, pl.ds(c * nbr, nbr)],
            send_sem=pick_send.at[c, p],
            recv_sem=pick_recv.at[c, p],
            device_id={"pool": p},
            device_id_type=MESH,
        )

    def choose(q, carry):
        pick[q] = got[place[q]]
        return carry

    lax.fori_loop(0, top * per, choose, 0)
    for k in range(per):
        blk[pool, k] = got[place[mine * per + k]]
    for c in range(spans):
        for p in range(top):

            @pl.when(pool != p)
            def _():
                pick_copy(p, c).start()

    def span(c, carry):
        for p in range(pools):

            @pl.when(pool != p)
            def _():
                pick_from(p, c).wait_recv()

        keys = nbr * slot_len
        scaling = HEAD ** (-0.5)
        at = pl.ds(pl.multiple_of(c * SPAN, SPAN), SPAN)
        rows = jnp.concatenate(
            [blk[p, c * nbr + n] for n in range(nbr) for p in range(pools)], axis=0
        ).astype(F32)
        cond = cond_ref[...].astype(F32)
        here = lax.broadcasted_iota(jnp.int32, cond.shape, 0) == c
        cond_row = jnp.sum(jnp.where(here, cond, 0.0), axis=0, keepdims=True)
        gain = gain_ref[...]
        x_full = rows + cond_row
        inv_rms = lax.rsqrt(jnp.mean(x_full * x_full, axis=-1, keepdims=True) + EPSILON)
        normed = x_full * inv_rms
        hidden = (normed * gain).astype(BF16)
        latent = dot_nn(hidden, wd_ref[...]).astype(BF16)
        encoded = (x_full + dot_nn(latent, wu_ref[...])).astype(BF16)
        for t in range(2 * hq // 512):
            cols = pl.ds(t * 512, 512)
            kv[:, cols] = dot_nn(encoded, wkv_ref[:, cols]).astype(BF16)

        slot = lax.broadcasted_iota(jnp.int32, (SPAN, keys), 1)
        bound = jnp.where(slot < slot_len, lens[c * nbr], lens[c * nbr + 1] + slot_len)
        usable = slot < bound

        def score(h):
            qs = pl.ds(h * HEAD, HEAD)
            vs = pl.ds(hq + h * HEAD, HEAD)
            s = dot_nt(q_ref[at, qs], kv[:, qs])
            dp = dot_nt(do_ref[at, qs], kv[:, vs])
            return s, dp

        def weigh(s, dp):
            s = jnp.where(usable, s * scaling, FLOOR)
            e = jnp.exp(s - jnp.max(s, axis=-1, keepdims=True))
            p = e * (1.0 / jnp.sum(e, axis=-1, keepdims=True))
            pdp = p * dp
            delta = jnp.sum(pdp, axis=-1, keepdims=True)
            return p.astype(BF16), (pdp - p * delta).astype(BF16)

        def finish(h, pb, ds):
            qs = pl.ds(h * HEAD, HEAD)
            vs = pl.ds(hq + h * HEAD, HEAD)
            out_ref[at, qs] = dot_nn(pb, kv[:, vs]).astype(BF16)
            dq_ref[at, qs] = (dot_nn(ds, kv[:, qs]) * scaling).astype(BF16)
            kvg[:, qs] = (dot_tn(ds, q_ref[at, qs]) * scaling).astype(BF16)
            kvg[:, vs] = dot_tn(pb, do_ref[at, qs]).astype(BF16)

        heads = hq // HEAD
        first, second = {}, {}
        for i in range(heads + 2 * STAGE):
            if i < heads:
                first[i] = score(i)
            if 0 <= i - STAGE < heads:
                second[i - STAGE] = weigh(*first.pop(i - STAGE))
            if 0 <= i - 2 * STAGE < heads:
                finish(i - 2 * STAGE, *second.pop(i - 2 * STAGE))

        enc_grad = dot_nt(kvg[...], wkv_ref[...]).astype(BF16)
        lat_grad = dot_nt(enc_grad, wu_ref[...]).astype(BF16)
        scaled = dot_nt(lat_grad, wd_ref[...]) * gain
        mean = jnp.mean(scaled * normed, axis=-1, keepdims=True)
        x_grad = enc_grad.astype(F32) + inv_rms * (scaled - normed * mean)
        cg_ref[pl.ds(c, 1), :] = jnp.sum(x_grad, axis=0, keepdims=True)
        ad_ref[:, :rank] += dot_tn(hidden, lat_grad)
        ad_ref[:, rank:] += dot_tn(enc_grad, latent)
        return carry

    def a_copy(d):
        to = lax.rem(me + d, columns)
        return pltpu.make_async_remote_copy(
            src_ref=part.at[to],
            dst_ref=lands.at[me],
            send_sem=a_send.at[d],
            recv_sem=a_recv.at[columns - d],
            device_id={"dp": to},
            device_id_type=MESH,
        )

    def b_copy(p):
        return pltpu.make_async_remote_copy(
            src_ref=held.at[p],
            dst_ref=tops.at[pool],
            send_sem=b_send.at[p],
            recv_sem=b_recv.at[pool],
            device_id={"pool": p},
            device_id_type=MESH,
        )

    def b_from(p):
        return pltpu.make_async_remote_copy(
            src_ref=held.at[p],
            dst_ref=tops.at[p],
            send_sem=b_send.at[p],
            recv_sem=b_recv.at[p],
            device_id={"pool": p},
            device_id_type=MESH,
        )

    @pl.when(is_dec)
    def _():
        for load in loads:
            load.wait()
        lax.fori_loop(0, spans, span, 0)
        piece = part.shape[2]
        for j in range(columns):
            for p in range(pools):
                part[j, p] = ad_ref[pl.ds((p * columns + j) * piece, piece), :].astype(BF16)
        each(lambda d: a_copy(d).start())
        lands[me] = part[me]

    each(lambda d: slot_copy(d).wait_send())
    for c in range(spans):
        for p in range(top):

            @pl.when(pool != p)
            def _():
                pick_copy(p, c).wait_send()

    @pl.when(is_dec)
    def _():
        each(lambda d: a_copy(d).wait())

        def add(j, total):
            return total + lands[j].astype(F32)

        held[...] = lax.fori_loop(1, columns, add, lands[0].astype(F32))
        for p in range(pools):

            @pl.when(pool != p)
            def _():
                b_copy(p).start()

            @pl.when(pool == p)
            def _():
                tops[p] = held[p]

        for p in range(pools):

            @pl.when(pool != p)
            def _():
                b_copy(p).wait_send()

    for p in range(top):

        @pl.when(pool != p)
        def _():
            b_from(p).wait_recv()

    total = tops[0]
    for p in range(1, top):
        total = total + tops[p]
    sum_ref[...] = total


def body(
    queries, cotangent, cond, nbr_owner, nbr_block, database, lengths, gain, w_down, w_up, w_kv
):
    pools = lax.axis_size("pool")
    columns = lax.axis_size("dp")
    tokens, hq = queries.shape[2:]
    spans, width = cond.shape[2:]
    nbr = nbr_owner.shape[3]
    blocks, slot_len = database.shape[2:4]
    rank = w_down.shape[1]
    per = spans * nbr
    quarter = slot_len // pools
    live = (pools - 1) * per
    piece = width // (pools * columns)
    dma = pltpu.SemaphoreType.DMA
    vmem = pl.BlockSpec(memory_space=pltpu.VMEM)
    smem = pl.BlockSpec(memory_space=pltpu.SMEM)
    where = pl.BlockSpec(memory_space=pl.ANY)
    attn_out, q_grad, cond_grad, adapter_grad = pl.pallas_call(
        functools.partial(whole_kernel, pools, columns),
        out_shape=(
            jax.ShapeDtypeStruct((tokens, hq), BF16),
            jax.ShapeDtypeStruct((tokens, hq), BF16),
            jax.ShapeDtypeStruct((spans, width), F32),
            jax.ShapeDtypeStruct((piece, 2 * rank), F32),
        ),
        in_specs=[smem, smem, smem, where, where, where, vmem, vmem, where, where, where],
        out_specs=(vmem, vmem, vmem, vmem),
        scratch_shapes=[
            pltpu.VMEM((1, 128), jnp.int32),
            pltpu.VMEM((columns, pools, 1, 128), jnp.int32),
            pltpu.SMEM((columns, pools, 1, 128), jnp.int32),
            pltpu.VMEM((columns, 128), jnp.int32),
            pltpu.SMEM((columns, 128), jnp.int32),
            pltpu.SMEM((live,), jnp.int32),
            pltpu.SMEM((per,), jnp.int32),
            pltpu.VMEM((blocks, quarter, width), BF16),
            pltpu.VMEM((columns, 2, quarter, width), BF16),
            pltpu.VMEM((2 * columns, quarter, width), BF16),
            pltpu.VMEM((live, quarter, width), BF16),
            pltpu.VMEM((pools, per, quarter, width), BF16),
            pltpu.VMEM((tokens, hq), BF16),
            pltpu.VMEM((tokens, hq), BF16),
            pltpu.VMEM((width, rank), BF16),
            pltpu.VMEM((rank, width), BF16),
            pltpu.VMEM((width, 2 * hq), BF16),
            pltpu.VMEM((nbr * slot_len, 2 * hq), BF16),
            pltpu.VMEM((nbr * slot_len, 2 * hq), BF16),
            pltpu.VMEM((width, 2 * rank), F32),
            pltpu.VMEM((columns, pools, piece, 2 * rank), BF16),
            pltpu.VMEM((columns, pools, piece, 2 * rank), BF16),
            pltpu.VMEM((pools, piece, 2 * rank), F32),
            pltpu.VMEM((pools, piece, 2 * rank), F32),
            dma((5,)),
            dma((3,)),
            dma((pools,)),
            dma,
            dma((pools,)),
            dma((pools,)),
            dma((columns,)),
            dma((columns,)),
            dma((columns,)),
            dma((columns,)),
            dma((spans, pools)),
            dma((spans, pools)),
            dma((columns,)),
            dma((columns,)),
            dma((pools,)),
            dma((pools,)),
        ],
        compiler_params=pltpu.CompilerParams(
            collective_id=0, has_side_effects=True, vmem_limit_bytes=60 << 20
        ),
        name="whole",
    )(
        nbr_owner.reshape(spans, nbr).T,
        nbr_block.reshape(spans, nbr).T,
        lengths.reshape(1, blocks),
        database.reshape(blocks, slot_len, width),
        queries.reshape(tokens, hq),
        cotangent.reshape(tokens, hq),
        cond.reshape(spans, width),
        gain.reshape(1, width),
        w_down,
        w_up,
        w_kv,
    )
    return (
        attn_out.reshape(1, 1, tokens, hq),
        q_grad.reshape(1, 1, tokens, hq),
        cond_grad.reshape(1, 1, spans, width),
        adapter_grad,
    )


def solution(mesh):
    return jax.shard_map(
        body,
        mesh=mesh,
        in_specs=(
            P("pool", "dp", None, None),
            P("pool", "dp", None, None),
            P("pool", "dp", None, None),
            P("pool", "dp", None, None),
            P("pool", "dp", None, None),
            P("pool", "dp", None, None, None),
            P("pool", "dp", None),
            P(),
            P(),
            P(),
            P(),
        ),
        out_specs=(
            P("pool", "dp", None, None),
            P("pool", "dp", None, None),
            P("pool", "dp", None, None),
            P(("pool", "dp"), None),
        ),
        check_vma=False,
    )
```

time: 192 us -> 98.7 us (0.51)
  waiting for transfers between devices: 71.8 us -> 0 us
  Pallas kernels: 50.9 us -> 91.8 us
  starting transfers between devices: 26.8 us -> 0 us
  blocking collectives: 24.4 us -> 0 us
  other arithmetic: 5.89 us -> 0 us
  local copies, waits for them, and re-layouts: 10.9 us -> 5.82 us
    all_to_all x4 -> x0, waiting for transfers between devices: 71.8 us -> none  [the longest x1 26.5 us: body(): got = lax.all_to_all(send, 'dp', split_axis=0, concat_axis=0, tiled=True)]
    pallas_call x1, Pallas kernels: 50.9 us -> 91.8 us  [body(): pl.pallas_call(functools.partial(whole_kernel, pools, columns), out_shape...]
    all_to_all x4 -> x0, starting transfers between devices: 26.8 us -> none  [the longest x1 11.5 us: body(): lax.all_to_all(meta, ('pool', 'dp'), split_axis=0, concat_axis=0, tiled=T...]
    all_to_all x1 -> x0, blocking collectives: 24.4 us -> none  [body(): lax.all_to_all(adapter, ('pool', 'dp'), split_axis=0, concat_axis=0, tile...]
    transpose x1 -> x0, local copies, waits for them, and re-layouts: 3.19 us -> none  [body(): db4 = jnp.swapaxes(db4, 0, 1)]
    unnamed x6 -> x8, local copies, waits for them, and re-layouts: 2.68 us -> 5.82 us
    concatenate x3 -> x0, other arithmetic: 2.39 us -> none  [the longest x1 1.06 us: body(): pick = jnp.concatenate([pick, pick[:1]], axis=0)]
    gather x3 -> x0, local copies, waits for them, and re-layouts: 1.92 us -> none  [the longest x1 0.68 us: body(): jnp.take(mine, slot_block, axis=0).reshape(columns, 2, quarter, enc_width)]
  transfers between devices with their start and end apart: 4 -> 0, of which waited for: 4 -> 0; matrix products, arithmetic and copies ran while one was open for 3% -> 0% of each run, Pallas kernels for 0% -> 0%
where the time goes in v5:
time: 98.7 us; the launch traced here: 98.3 us
  Pallas kernels  91.8 us (93%)
  local copies, waits for them, and re-layouts  5.82 us (6%)
    pallas_call x1, Pallas kernels, body(): pl.pallas_call(functools.partial(whole_kernel, pools, columns), out_shape...  91.8 us
    unnamed x8, local copies, waits for them, and re-layouts  5.82 us

profile of v5, /device:TPU:1, one launch (start us, length us, event | category | flops | bytes accessed | tf_op | source)
XLA Modules:
  0.0 98.3 jit_solution(8551464959255941022)
XLA Ops:
  0.6 91.8 %whole.1 = (bf16[256,2048]{1,0:T(8,128)(2,1)}, bf16[256,2048]{1,0:T(8,128)(2,1)}, f32[4,512]{1,0:T(4,128)}, f32[4,512]{1,0:T(4,128)}) custom-call(s32[2,4]{1,0:T(2,128)} %bitcast.23, s32[2,4]{1,0:T(2,128)} %bitcast.24, s32[1,16]{1,0:T(1,128)} %bitcast.25, bf16[16,128,512]{2,1,0:T(8,128)(2,1)} %bitcast.15, bf16[256,2048]{1,0:T(8,128)(2,1)} %bitcast.18, ...), custom_call_target="tpu_custom_call" | custom-call | tf_op jit(solution)/shard_map/whole/pallas_call | solution.py:434
  92.4 0.0 copy-start.1
  92.4 0.0 copy-start
  92.4 2.3 %copy.19 = bf16[1,1,256,2048]{3,2,1,0:T(8,128)(2,1)} copy(bf16[1,1,256,2048]{3,2,1,0:T(8,128)(2,1)} %bitcast.17) | data formatting | bytes 2097152
  94.8 2.3 %copy.20 = bf16[1,1,256,2048]{3,2,1,0:T(8,128)(2,1)} copy(bf16[1,1,256,2048]{3,2,1,0:T(8,128)(2,1)} %bitcast.16) | data formatting | bytes 2097152
  97.1 0.0 copy-done.1
  97.1 0.6 copy.21
  97.7 0.0 copy-done
  97.7 0.6 copy.22
Async XLA Ops:
  92.4 4.6 %copy-start.1 = (f32[4,512]{1,0:T(4,128)S(1)}, f32[4,512]{1,0:T(4,128)}, u32[]{:S(2)}) copy-start(f32[4,512]{1,0:T(4,128)} %get-tuple-element.10) | copy-start | bytes 24580
  92.4 5.2 %copy-start = (f32[4,512]{1,0:T(4,128)S(1)}, f32[4,512]{1,0:T(4,128)}, u32[]{:S(2)}) copy-start(f32[4,512]{1,0:T(4,128)} %get-tuple-element.19) | copy-start | bytes 24580

commit v6 on v5

--- a/solution.py
+++ b/solution.py
@@ -51,10 +51,10 @@
     pools, columns,
     owner_ref, block_ref, len_ref, db_ref, q_hbm, do_hbm, cond_ref, gain_ref, wd_hbm, wu_hbm,
     wkv_hbm,
-    out_ref, dq_ref, cg_ref, sum_ref,
-    row, metas, smeta, found, table, place, lens, share, send, got, pick, blk,
+    out_hbm, dq_hbm, cg_ref, sum_ref,
+    out_ref, dq_ref, row, metas, smeta, found, table, place, lens, share, send, got, pick, blk,
     q_ref, do_ref, wd_ref, wu_ref, wkv_ref, kv, kvg, ad_ref, part, lands, held, tops,
-    load_sem, local_sem, base_send, base_recv, row_send, row_recv, meta_send, meta_recv,
+    load_sem, store_sem, local_sem, base_send, base_recv, row_send, row_recv, meta_send, meta_recv,
     slot_send, slot_recv, pick_send, pick_recv, a_send, a_recv, b_send, b_recv,
 ):
     pool, me = lax.axis_index("pool"), lax.axis_index("dp")
@@ -110,6 +110,30 @@
 
     for d in range(1, pools):
         row_copy(d).start()
+
+    early = blocks // 4
+    halves = (pl.ds(0, early), pl.ds(early, blocks - early))
+
+    def base_copy(p, half):
+        return pltpu.make_async_remote_copy(
+            src_ref=db_ref.at[halves[half], pl.ds(p * quarter, quarter), :],
+            dst_ref=share.at[halves[half]],
+            send_sem=base_send.at[half, p],
+            recv_sem=base_recv.at[half],
+            device_id={"pool": p},
+            device_id_type=MESH,
+        )
+
+    base_own = pltpu.make_async_copy(
+        db_ref.at[:, pl.ds(top * quarter, quarter), :], share, local_sem.at[0]
+    )
+
+    @pl.when(is_enc)
+    def _():
+        for p in range(top):
+            base_copy(p, 0).start()
+        base_own.start()
+
     for d in range(1, pools):
         row_copy(d).wait()
 
@@ -125,25 +149,11 @@
 
     each(lambda d: meta_copy(d).start())
 
-    def base_copy(p):
-        return pltpu.make_async_remote_copy(
-            src_ref=db_ref.at[:, pl.ds(p * quarter, quarter), :],
-            dst_ref=share,
-            send_sem=base_send.at[p],
-            recv_sem=base_recv,
-            device_id={"pool": p},
-            device_id_type=MESH,
-        )
-
-    base_own = pltpu.make_async_copy(
-        db_ref.at[:, pl.ds(top * quarter, quarter), :], share, local_sem.at[0]
-    )
-
     @pl.when(is_enc)
     def _():
         for p in range(top):
-            base_copy(p).start()
-        base_own.start()
+            base_copy(p, 1).start()
+
 
     each(lambda d: meta_copy(d).wait())
     to_scalar = pltpu.make_async_copy(metas, smeta, local_sem.at[1])
@@ -171,7 +181,8 @@
 
     @pl.when(is_dec)
     def _():
-        base_copy(0).wait_recv()
+        base_copy(0, 0).wait_recv()
+        base_copy(0, 1).wait_recv()
 
     def fill(j, carry):
         for r in range(2):
@@ -209,12 +220,23 @@
     ad_ref[...] = jnp.zeros_like(ad_ref)
     cg_ref[...] = jnp.zeros_like(cg_ref)
 
+    def stores(c):
+        at = pl.ds(pl.multiple_of(c * SPAN, SPAN), SPAN)
+        return (
+            pltpu.make_async_copy(out_ref.at[at], out_hbm.at[at], store_sem.at[c, 0]),
+            pltpu.make_async_copy(dq_ref.at[at], dq_hbm.at[at], store_sem.at[c, 1]),
+        )
+
     @pl.when(is_enc)
     def _():
         out_ref[...] = jnp.zeros_like(out_ref)
         dq_ref[...] = jnp.zeros_like(dq_ref)
         for p in range(top):
-            base_copy(p).wait_send()
+            for part_of in range(2):
+                base_copy(p, part_of).wait_send()
+        for c in range(spans):
+            for store in stores(c):
+                store.start()
 
     each(lambda d: slot_copy(d).wait_recv())
 
@@ -258,6 +280,11 @@
             @pl.when(pool != p)
             def _():
                 pick_from(p, c).wait_recv()
+
+        @pl.when(c > 0)
+        def _():
+            for store in stores(c - 1):
+                store.start()
 
         keys = nbr * slot_len
         scaling = HEAD ** (-0.5)
@@ -362,6 +389,8 @@
         for load in loads:
             load.wait()
         lax.fori_loop(0, spans, span, 0)
+        for store in stores(spans - 1):
+            store.start()
         piece = part.shape[2]
         for j in range(columns):
             for p in range(pools):
@@ -369,6 +398,10 @@
         each(lambda d: a_copy(d).start())
         lands[me] = part[me]
 
+    for c in range(spans):
+        for store in stores(c):
+            store.wait()
+
     each(lambda d: slot_copy(d).wait_send())
     for c in range(spans):
         for p in range(top):
@@ -411,6 +444,45 @@
     for p in range(1, top):
         total = total + tops[p]
     sum_ref[...] = total
+
+
+def flush_kernel(chunks, *refs):
+    n = len(chunks)
+    sources, targets, bounces = refs[:n], refs[n : 2 * n], refs[2 * n : 3 * n]
+    in_sem, out_sem = refs[3 * n :]
+    steps = []
+    for i in range(n):
+        size = sources[i].shape[0] // chunks[i]
+        for t in range(chunks[i]):
+            at = pl.ds(t * size, size)
+            k = len(steps)
+            steps.append(
+                (
+                    pltpu.make_async_copy(sources[i].at[at], bounces[i].at[at], in_sem.at[k]),
+                    pltpu.make_async_copy(bounces[i].at[at], targets[i].at[at], out_sem.at[k]),
+                )
+            )
+    for load, _ in steps:
+        load.start()
+    for load, store in steps:
+        load.wait()
+        store.start()
+    for _, store in steps:
+        store.wait()
+
+
+def flush(chunks, *arrays):
+    where = pl.BlockSpec(memory_space=pl.ANY)
+    return pl.pallas_call(
+        functools.partial(flush_kernel, chunks),
+        out_shape=tuple(jax.ShapeDtypeStruct(a.shape, a.dtype) for a in arrays),
+        in_specs=[where] * len(arrays),
+        out_specs=(where,) * len(arrays),
+        scratch_shapes=[pltpu.VMEM(a.shape, a.dtype) for a in arrays]
+        + [pltpu.SemaphoreType.DMA((sum(chunks),))] * 2,
+        compiler_params=pltpu.CompilerParams(vmem_limit_bytes=60 << 20),
+        name="flush",
+    )(*arrays)
 
 
 def body(
@@ -440,8 +512,10 @@
             jax.ShapeDtypeStruct((piece, 2 * rank), F32),
         ),
         in_specs=[smem, smem, smem, where, where, where, vmem, vmem, where, where, where],
-        out_specs=(vmem, vmem, vmem, vmem),
+        out_specs=(where, where, vmem, vmem),
         scratch_shapes=[
+            pltpu.VMEM((tokens, hq), BF16),
+            pltpu.VMEM((tokens, hq), BF16),
             pltpu.VMEM((1, 128), jnp.int32),
             pltpu.VMEM((columns, pools, 1, 128), jnp.int32),
             pltpu.SMEM((columns, pools, 1, 128), jnp.int32),
@@ -467,9 +541,10 @@
             pltpu.VMEM((pools, piece, 2 * rank), F32),
             pltpu.VMEM((pools, piece, 2 * rank), F32),
             dma((5,)),
+            dma((spans, 2)),
             dma((3,)),
-            dma((pools,)),
-            dma,
+            dma((2, pools)),
+            dma((2,)),
             dma((pools,)),
             dma((pools,)),
             dma((columns,)),
@@ -500,6 +575,9 @@
         w_up,
         w_kv,
     )
+    attn_out, q_grad, cond_grad, adapter_grad = flush(
+        (4, 4, 1, 1), attn_out, q_grad, cond_grad, adapter_grad
+    )
     return (
         attn_out.reshape(1, 1, tokens, hq),
         q_grad.reshape(1, 1, tokens, hq),

time: 98.7 us -> 97.5 us (0.988); the launches traced: 98.3 us -> 95.9 us
  local copies, waits for them, and re-layouts: 5.82 us -> 0 us
  Pallas kernels: 91.8 us -> 95.3 us
    unnamed x8 -> x0, local copies, waits for them, and re-layouts: 5.82 us -> none
    pallas_call x0 -> x1, Pallas kernels: none -> 2.44 us  [flush(): pl.pallas_call(functools.partial(flush_kernel, chunks), out_shape=tuple((...]
    pallas_call x1, Pallas kernels: 91.8 us -> 92.8 us  [body(): pl.pallas_call(functools.partial(whole_kernel, pools, columns), out_shape...]
where the time goes in v6:
time: 97.5 us; the launch traced here: 95.9 us
  Pallas kernels  95.3 us (98%)
    pallas_call x1, Pallas kernels, body(): pl.pallas_call(functools.partial(whole_kernel, pools, columns), out_shape...  92.8 us
    pallas_call x1, Pallas kernels, flush(): pl.pallas_call(functools.partial(flush_kernel, chunks), out_shape=tuple((...  2.44 us

profile of v6, /device:TPU:1, one launch (start us, length us, event | category | flops | bytes accessed | tf_op | source)
XLA Modules:
  0.0 95.9 jit_solution(3078309710614866535)
XLA Ops:
  0.6 92.8 %whole.1 = (bf16[256,2048]{1,0:T(8,128)(2,1)}, bf16[256,2048]{1,0:T(8,128)(2,1)}, f32[4,512]{1,0:T(4,128)}, f32[4,512]{1,0:T(4,128)}) custom-call(s32[2,4]{1,0:T(2,128)} %bitcast.20, s32[2,4]{1,0:T(2,128)} %bitcast.21, s32[1,16]{1,0:T(1,128)} %bitcast.22, bf16[16,128,512]{2,1,0:T(8,128)(2,1)} %bitcast.15, bf16[256,2048]{1,0:T(8,128)(2,1)} %bitcast.16, ...), custom_call_target="tpu_custom_call" | custom-call | tf_op jit(solution)/shard_map/whole/pallas_call | solution.py:506
  93.5 2.4 %flush.1 = (bf16[256,2048]{1,0:T(8,128)(2,1)}, bf16[256,2048]{1,0:T(8,128)(2,1)}, f32[4,512]{1,0:T(4,128)}, f32[4,512]{1,0:T(4,128)}) custom-call(bf16[256,2048]{1,0:T(8,128)(2,1)} %get-tuple-element.12.refs_0_, bf16[256,2048]{1,0:T(8,128)(2,1)} %get-tuple-element.13.refs_1_, f32[4,512]{1,0:T(4,128)} %get-tuple-element.14.refs_2_, ...), custom_call_target="tpu_custom_call" | custom-call | tf_op jit(solution)/shard_map/flush/pallas_call | solution.py:476

commit v7 on v6

--- a/solution.py
+++ b/solution.py
@@ -12,6 +12,8 @@
 EPSILON = 1e-06
 FLOOR = -1e30
 STAGE = 4
+GRID = (4, 2, 4)
+ORDER = ((3, 1, 1), (2, 0, 2), (1, 1, 0), (1, 0, 3), (3, 0, 3), (0, 0, 2), (0, 1, 2), (3, 1, 3), (1, 0, 0), (2, 0, 1), (1, 0, 2), (2, 1, 0), (3, 1, 2), (1, 1, 2), (2, 1, 2), (0, 0, 1), (2, 1, 1), (3, 0, 0), (0, 1, 3), (1, 1, 1), (2, 1, 3), (1, 1, 3), (2, 0, 0), (0, 1, 0), (1, 0, 1), (0, 0, 3), (3, 0, 1), (3, 0, 2), (3, 1, 0), (2, 0, 3), (0, 1, 1))
 F32 = jnp.float32
 BF16 = jnp.bfloat16
 MESH = pl.DeviceIdType.MESH
@@ -27,6 +29,12 @@
 
 def dot_tn(a, b):
     return lax.dot_general(a, b, (((0,), (0,)), ((), ())), preferred_element_type=F32)
+
+
+def shifted(me, step):
+    z, x, y = me // (GRID[1] * GRID[2]), lax.rem(me // GRID[2], GRID[1]), lax.rem(me, GRID[2])
+    z, x, y = (lax.rem(c + d, n) for c, d, n in zip((z, x, y), step, GRID))
+    return (z * GRID[1] + x) * GRID[2] + y
 
 
 def greet(pools, columns):
@@ -194,17 +202,18 @@
         got[2 * me + r] = share[table[me, r]]
 
     def slot_copy(d):
-        to = lax.rem(me + d, columns)
+        to = shifted(me, ORDER[d])
         return pltpu.make_async_remote_copy(
             src_ref=send.at[to],
             dst_ref=got.at[pl.ds(2 * me, 2)],
             send_sem=slot_send.at[d],
-            recv_sem=slot_recv.at[columns - d],
+            recv_sem=slot_recv.at[d],
             device_id={"dp": to},
             device_id_type=MESH,
         )
 
-    each(lambda d: slot_copy(d).start())
+    for d in range(columns - 1):
+        slot_copy(d).start()
 
     to_scalar.wait()
     names = [smeta[me, q // per, 0, q % per] for q in range(top * per)]
@@ -238,7 +247,8 @@
             for store in stores(c):
                 store.start()
 
-    each(lambda d: slot_copy(d).wait_recv())
+    for d in range(columns - 1):
+        slot_copy(d).wait_recv()
 
     def pick_copy(p, c):
         return pltpu.make_async_remote_copy(
@@ -354,12 +364,12 @@
         return carry
 
     def a_copy(d):
-        to = lax.rem(me + d, columns)
+        to = shifted(me, ORDER[d])
         return pltpu.make_async_remote_copy(
             src_ref=part.at[to],
             dst_ref=lands.at[me],
             send_sem=a_send.at[d],
-            recv_sem=a_recv.at[columns - d],
+            recv_sem=a_recv.at[d],
             device_id={"dp": to},
             device_id_type=MESH,
         )
@@ -395,14 +405,16 @@
         for j in range(columns):
             for p in range(pools):
                 part[j, p] = ad_ref[pl.ds((p * columns + j) * piece, piece), :].astype(BF16)
-        each(lambda d: a_copy(d).start())
+        for d in range(columns - 1):
+            a_copy(d).start()
         lands[me] = part[me]
 
     for c in range(spans):
         for store in stores(c):
             store.wait()
 
-    each(lambda d: slot_copy(d).wait_send())
+    for d in range(columns - 1):
+        slot_copy(d).wait_send()
     for c in range(spans):
         for p in range(top):
 
@@ -412,7 +424,8 @@
 
     @pl.when(is_dec)
     def _():
-        each(lambda d: a_copy(d).wait())
+        for d in range(columns - 1):
+            a_copy(d).wait()
 
         def add(j, total):
             return total + lands[j].astype(F32)

time: 97.5 us -> 90.9 us (0.932); the launches traced: 95.9 us -> 90.7 us
  Pallas kernels: 95.3 us -> 90 us
    pallas_call x1, Pallas kernels: 92.8 us -> 87.6 us  [body(): pl.pallas_call(functools.partial(whole_kernel, pools, columns), out_shape...]
where the time goes in v7:
time: 90.9 us; the launch traced here: 90.7 us
  Pallas kernels  90 us (99%)
    pallas_call x1, Pallas kernels, body(): pl.pallas_call(functools.partial(whole_kernel, pools, columns), out_shape...  87.6 us
    pallas_call x1, Pallas kernels, flush(): pl.pallas_call(functools.partial(flush_kernel, chunks), out_shape=tuple((...  2.44 us

profile of v7, /device:TPU:1, one launch (start us, length us, event | category | flops | bytes accessed | tf_op | source)
XLA Modules:
  0.0 90.7 jit_solution(1948734815646799811)
XLA Ops:
  0.6 87.6 %whole.1 = (bf16[256,2048]{1,0:T(8,128)(2,1)}, bf16[256,2048]{1,0:T(8,128)(2,1)}, f32[4,512]{1,0:T(4,128)}, f32[4,512]{1,0:T(4,128)}) custom-call(s32[2,4]{1,0:T(2,128)} %bitcast.20, s32[2,4]{1,0:T(2,128)} %bitcast.21, s32[1,16]{1,0:T(1,128)} %bitcast.22, bf16[16,128,512]{2,1,0:T(8,128)(2,1)} %bitcast.15, bf16[256,2048]{1,0:T(8,128)(2,1)} %bitcast.16, ...), custom_call_target="tpu_custom_call" | custom-call | tf_op jit(solution)/shard_map/whole/pallas_call | solution.py:519
  88.2 2.4 %flush.1 = (bf16[256,2048]{1,0:T(8,128)(2,1)}, bf16[256,2048]{1,0:T(8,128)(2,1)}, f32[4,512]{1,0:T(4,128)}, f32[4,512]{1,0:T(4,128)}) custom-call(bf16[256,2048]{1,0:T(8,128)(2,1)} %get-tuple-element.12.refs_0_, bf16[256,2048]{1,0:T(8,128)(2,1)} %get-tuple-element.13.refs_1_, f32[4,512]{1,0:T(4,128)} %get-tuple-element.14.refs_2_, ...), custom_call_target="tpu_custom_call" | custom-call | tf_op jit(solution)/shard_map/flush/pallas_call | solution.py:489

commit v8 on v7

--- a/solution.py
+++ b/solution.py
@@ -11,7 +11,7 @@
 SPAN = 64
 EPSILON = 1e-06
 FLOOR = -1e30
-STAGE = 4
+STAGE = 6
 GRID = (4, 2, 4)
 ORDER = ((3, 1, 1), (2, 0, 2), (1, 1, 0), (1, 0, 3), (3, 0, 3), (0, 0, 2), (0, 1, 2), (3, 1, 3), (1, 0, 0), (2, 0, 1), (1, 0, 2), (2, 1, 0), (3, 1, 2), (1, 1, 2), (2, 1, 2), (0, 0, 1), (2, 1, 1), (3, 0, 0), (0, 1, 3), (1, 1, 1), (2, 1, 3), (1, 1, 3), (2, 0, 0), (0, 1, 0), (1, 0, 1), (0, 0, 3), (3, 0, 1), (3, 0, 2), (3, 1, 0), (2, 0, 3), (0, 1, 1))
 F32 = jnp.float32
@@ -62,7 +62,7 @@
     out_hbm, dq_hbm, cg_ref, sum_ref,
     out_ref, dq_ref, row, metas, smeta, found, table, place, lens, share, send, got, pick, blk,
     q_ref, do_ref, wd_ref, wu_ref, wkv_ref, kv, kvg, ad_ref, part, lands, held, tops,
-    load_sem, store_sem, local_sem, base_send, base_recv, row_send, row_recv, meta_send, meta_recv,
+    load_sem, store_sem, local_sem, base_send, base_recv, row_send, row_recv, meta_send, meta_recv, hand_sem,
     slot_send, slot_recv, pick_send, pick_recv, a_send, a_recv, b_send, b_recv,
 ):
     pool, me = lax.axis_index("pool"), lax.axis_index("dp")
@@ -103,7 +103,11 @@
     for k in range(blocks):
         line = jnp.where(lane == 2 * per + k, len_ref[0, k], line)
     row[...] = line
-    metas[me, pool] = line
+
+    @pl.when(is_dec)
+    def _():
+        metas[me, pool] = line
+
     greet(pools, columns)
 
     def row_copy(d):
@@ -117,7 +121,10 @@
         )
 
     for d in range(1, pools):
-        row_copy(d).start()
+
+        @pl.when(lax.rem(pool + d, pools) != top)
+        def _():
+            row_copy(d).start()
 
     early = blocks // 4
     halves = (pl.ds(0, early), pl.ds(early, blocks - early))
@@ -138,12 +145,20 @@
 
     @pl.when(is_enc)
     def _():
-        for p in range(top):
-            base_copy(p, 0).start()
         base_own.start()
+        for p in (top - 1,) + tuple(range(top - 1)):
+            for half in range(2):
+                base_copy(p, half).start()
 
     for d in range(1, pools):
-        row_copy(d).wait()
+
+        @pl.when(lax.rem(pool + d, pools) != top)
+        def _():
+            row_copy(d).wait_send()
+
+        @pl.when(is_dec)
+        def _():
+            row_copy(d).wait_recv()
 
     def meta_copy(d):
         return pltpu.make_async_remote_copy(
@@ -155,17 +170,29 @@
             device_id_type=MESH,
         )
 
-    each(lambda d: meta_copy(d).start())
+    hand = pltpu.make_async_remote_copy(
+        src_ref=metas,
+        dst_ref=metas,
+        send_sem=hand_sem.at[0],
+        recv_sem=hand_sem.at[1],
+        device_id={"pool": top},
+        device_id_type=MESH,
+    )
+
+    @pl.when(is_dec)
+    def _():
+        each(lambda d: meta_copy(d).start())
+        each(lambda d: meta_copy(d).wait())
+
+    @pl.when(pool == top - 1)
+    def _():
+        hand.start()
 
     @pl.when(is_enc)
     def _():
-        for p in range(top):
-            base_copy(p, 1).start()
-
-
-    each(lambda d: meta_copy(d).wait())
+        hand.wait_recv()
+
     to_scalar = pltpu.make_async_copy(metas, smeta, local_sem.at[1])
-    to_scalar.start()
 
     lanes = lax.broadcasted_iota(jnp.int32, (columns, 128), 1)
     least = jnp.full((columns, 128), blocks << 16, jnp.int32)
@@ -182,6 +209,7 @@
     to_table = pltpu.make_async_copy(found, table, local_sem.at[2])
     to_table.start()
     to_table.wait()
+    to_scalar.start()
 
     @pl.when(is_enc)
     def _():
@@ -191,15 +219,6 @@
     def _():
         base_copy(0, 0).wait_recv()
         base_copy(0, 1).wait_recv()
-
-    def fill(j, carry):
-        for r in range(2):
-            send[j, r] = share[table[j, r]]
-        return carry
-
-    lax.fori_loop(0, columns, fill, 0)
-    for r in range(2):
-        got[2 * me + r] = share[table[me, r]]
 
     def slot_copy(d):
         to = shifted(me, ORDER[d])
@@ -212,8 +231,23 @@
             device_id_type=MESH,
         )
 
+    def fill(d):
+        to = shifted(me, ORDER[d])
+        for r in range(2):
+            send[to, r] = share[table[to, r]]
+
     for d in range(columns - 1):
+        fill(d)
+        if d >= 2:
+            slot_copy(d - 2).start()
+    for r in range(2):
+        got[2 * me + r] = share[table[me, r]]
+    for d in range(columns - 3, columns - 1):
         slot_copy(d).start()
+
+    @pl.when(pool == top - 1)
+    def _():
+        hand.wait_send()
 
     to_scalar.wait()
     names = [smeta[me, q // per, 0, q % per] for q in range(top * per)]
@@ -270,19 +304,25 @@
             device_id_type=MESH,
         )
 
-    def choose(q, carry):
-        pick[q] = got[place[q]]
-        return carry
-
-    lax.fori_loop(0, top * per, choose, 0)
-    for k in range(per):
-        blk[pool, k] = got[place[mine * per + k]]
-    for c in range(spans):
+    def choose(c):
+        for n in range(nbr):
+            k = c * nbr + n
+            for p in range(top):
+                pick[p * per + k] = got[place[p * per + k]]
+            blk[pool, k] = got[place[mine * per + k]]
+
+    def deliver(c):
         for p in range(top):
 
             @pl.when(pool != p)
             def _():
                 pick_copy(p, c).start()
+
+    choose(0)
+    for c in range(1, spans):
+        choose(c)
+        deliver(c - 1)
+    deliver(spans - 1)
 
     def span(c, carry):
         for p in range(pools):
@@ -562,6 +602,7 @@
             dma((pools,)),
             dma((columns,)),
             dma((columns,)),
+            dma((2,)),
             dma((columns,)),
             dma((columns,)),
             dma((spans, pools)),

time: 90.9 us -> 89.9 us (0.989)
  Pallas kernels: 90 us -> 88.5 us
    pallas_call x1, Pallas kernels: 87.6 us -> 86 us  [body(): pl.pallas_call(functools.partial(whole_kernel, pools, columns), out_shape...]
where the time goes in v8:
time: 89.9 us; the launch traced here: 89.1 us
  Pallas kernels  88.5 us (98%)
    pallas_call x1, Pallas kernels, body(): pl.pallas_call(functools.partial(whole_kernel, pools, columns), out_shape...  86 us
    pallas_call x1, Pallas kernels, flush(): pl.pallas_call(functools.partial(flush_kernel, chunks), out_shape=tuple((...  2.44 us

profile of v8, /device:TPU:1, one launch (start us, length us, event | category | flops | bytes accessed | tf_op | source)
XLA Modules:
  0.0 89.1 jit_solution(17124678746868169422)
XLA Ops:
  0.6 86.0 %whole.1 = (bf16[256,2048]{1,0:T(8,128)(2,1)}, bf16[256,2048]{1,0:T(8,128)(2,1)}, f32[4,512]{1,0:T(4,128)}, f32[4,512]{1,0:T(4,128)}) custom-call(s32[2,4]{1,0:T(2,128)} %bitcast.20, s32[2,4]{1,0:T(2,128)} %bitcast.21, s32[1,16]{1,0:T(1,128)} %bitcast.22, bf16[16,128,512]{2,1,0:T(8,128)(2,1)} %bitcast.15, bf16[256,2048]{1,0:T(8,128)(2,1)} %bitcast.16, ...), custom_call_target="tpu_custom_call" | custom-call | tf_op jit(solution)/shard_map/whole/pallas_call | solution.py:559
  86.7 2.4 %flush.1 = (bf16[256,2048]{1,0:T(8,128)(2,1)}, bf16[256,2048]{1,0:T(8,128)(2,1)}, f32[4,512]{1,0:T(4,128)}, f32[4,512]{1,0:T(4,128)}) custom-call(bf16[256,2048]{1,0:T(8,128)(2,1)} %get-tuple-element.12.refs_0_, bf16[256,2048]{1,0:T(8,128)(2,1)} %get-tuple-element.13.refs_1_, f32[4,512]{1,0:T(4,128)} %get-tuple-element.14.refs_2_, ...), custom_call_target="tpu_custom_call" | custom-call | tf_op jit(solution)/shard_map/flush/pallas_call | solution.py:529

commit v9 on v8

--- a/solution.py
+++ b/solution.py
@@ -630,7 +630,7 @@
         w_kv,
     )
     attn_out, q_grad, cond_grad, adapter_grad = flush(
-        (4, 4, 1, 1), attn_out, q_grad, cond_grad, adapter_grad
+        (8, 8, 1, 1), attn_out, q_grad, cond_grad, adapter_grad
     )
     return (
         attn_out.reshape(1, 1, tokens, hq),

time: 89.9 us -> 90.1 us (level)
  no operation moved by 1% of the time
where the time goes in v9:
time: 90.1 us; the launch traced here: 89.3 us
  Pallas kernels  88.6 us (98%)
    pallas_call x1, Pallas kernels, body(): pl.pallas_call(functools.partial(whole_kernel, pools, columns), out_shape...  86 us
    pallas_call x1, Pallas kernels, flush(): pl.pallas_call(functools.partial(flush_kernel, chunks), out_shape=tuple((...  2.61 us

profile of v9, /device:TPU:1, one launch (start us, length us, event | category | flops | bytes accessed | tf_op | source)
XLA Modules:
  0.0 89.3 jit_solution(5358807817002160920)
XLA Ops:
  0.6 86.0 %whole.1 = (bf16[256,2048]{1,0:T(8,128)(2,1)}, bf16[256,2048]{1,0:T(8,128)(2,1)}, f32[4,512]{1,0:T(4,128)}, f32[4,512]{1,0:T(4,128)}) custom-call(s32[2,4]{1,0:T(2,128)} %bitcast.20, s32[2,4]{1,0:T(2,128)} %bitcast.21, s32[1,16]{1,0:T(1,128)} %bitcast.22, bf16[16,128,512]{2,1,0:T(8,128)(2,1)} %bitcast.15, bf16[256,2048]{1,0:T(8,128)(2,1)} %bitcast.16, ...), custom_call_target="tpu_custom_call" | custom-call | tf_op jit(solution)/shard_map/whole/pallas_call | solution.py:559
  86.7 2.6 %flush.1 = (bf16[256,2048]{1,0:T(8,128)(2,1)}, bf16[256,2048]{1,0:T(8,128)(2,1)}, f32[4,512]{1,0:T(4,128)}, f32[4,512]{1,0:T(4,128)}) custom-call(bf16[256,2048]{1,0:T(8,128)(2,1)} %get-tuple-element.12.refs_0_, bf16[256,2048]{1,0:T(8,128)(2,1)} %get-tuple-element.13.refs_1_, f32[4,512]{1,0:T(4,128)} %get-tuple-element.14.refs_2_, ...), custom_call_target="tpu_custom_call" | custom-call | tf_op jit(solution)/shard_map/flush/pallas_call | solution.py:529
